TPU v7x, 32 devices: a whole 2x2x4 slice. The times are simulated.
32 devices in a mesh: dp: 8 (over z, x), mp: 4 (over y, core).
Axes of the slice: x: 2, y: 2, z: 4, core: 2. Of those that a mesh axis runs over, the one named last changes fastest.
Arguments:
- patches: bfloat16 [32000, 768], P(('dp', 'mp')), may hold values from -6 to 6
- dataset_id: int32 [160], P('dp'), may hold values from 0 to 7
- patch_masks: int32 [8, 200], replicated, may hold values 0 or 1
- mask_tokens: bfloat16 [8, 768], replicated, may hold values from -6 to 6
- key_mask: int32 [160, 200], P('dp'), may hold values from 0 to 1, as said below
- bias_index: int32 [200, 200], replicated, may hold values from 0 to 731
- norm1_gain: float32 [768], replicated, may hold values from 0.5 to 1.5
- norm1_shift: float32 [768], replicated, may hold values from -1.8 to 1.8
- qkv_weight: bfloat16 [768, 3, 768], P(None, None, 'mp'), may hold values from -0.21875 to 0.21875
- query_bias: bfloat16 [768], P('mp'), may hold values from -3 to 3
- value_bias: bfloat16 [768], P('mp'), may hold values from -3 to 3
- bias_table: bfloat16 [732, 12], P(None, 'mp'), may hold values from -5 to 5
- out_weight: bfloat16 [768, 768], P('mp'), may hold values from -1.75 to 1.75
- out_bias: float32 [768], replicated, may hold values from -1.8 to 1.8
- gamma_attn: float32 [768], replicated, may hold values from 0.5 to 2
- norm2_gain: float32 [768], replicated, may hold values from 0.5 to 1.5
- norm2_shift: float32 [768], replicated, may hold values from -1.8 to 1.8
- up_weight: bfloat16 [768, 3072], P(None, 'mp'), may hold values from -0.21875 to 0.21875
- up_bias: bfloat16 [3072], P('mp'), may hold values from -3 to 3
- down_weight: bfloat16 [3072, 768], P('mp'), may hold values from -0.109375 to 0.109375
- down_bias: float32 [768], replicated, may hold values from -1.8 to 1.8
- gamma_mlp: float32 [768], replicated, may hold values from 0.5 to 2
- cotangent: bfloat16 [32000, 768], P(('dp', 'mp')), may hold values from -6 to 6
Outputs:
- output: bfloat16 [32000, 768], P(('dp', 'mp'))
- patch_grad: float32 [32000, 768], P(('dp', 'mp'))
- token_grad: float32 [8, 768], replicated
- norm1_gain_grad: float32 [768], replicated
- norm1_shift_grad: float32 [768], replicated
- qkv_grad: float32 [768, 3, 768], P(None, None, 'mp')
- query_bias_grad: float32 [768], P('mp')
- value_bias_grad: float32 [768], P('mp')
- table_grad: float32 [732, 12], P(None, 'mp')
- out_weight_grad: float32 [768, 768], P('mp')
- out_bias_grad: float32 [768], replicated
- gamma_attn_grad: float32 [768], replicated
- norm2_gain_grad: float32 [768], replicated
- norm2_shift_grad: float32 [768], replicated
- up_weight_grad: float32 [768, 3072], P(None, 'mp')
- up_bias_grad: float32 [3072], P('mp')
- down_weight_grad: float32 [3072, 768], P('mp')
- down_bias_grad: float32 [768], replicated
- gamma_mlp_grad: float32 [768], replicated
Inputs may be any that keep to these rules, and one draw needn't show every extreme that they name: `key_mask`: each row holds ones on a prefix of its positions and zeros after it; the first position is always one.
All inputs are finite; a program needn't handle non-finite values.
Results may differ from a plain program's by a relative error of at most 0.013.
The roundings to bfloat16 on the way count: a program that leaves them out, or rounds other values in their place, can miss the bound.
Values may be sent and summed in bfloat16 or wider, within the bound.
No kernel may reach another device: no remote copies, remote signals or barrier semaphores. Data moves between devices by JAX's collectives and lax.ppermute only.
A program may use at most 192 MiB of HBM per device.

v0:
```python
import functools

import jax
import jax.numpy as jnp
from jax import lax
from jax.experimental import pallas as pl
from jax.experimental.pallas import tpu as pltpu
from jax.sharding import PartitionSpec as P

HEAD = 64
SEQ = 200
GROUPS = 8
LANES = 128
BF = jnp.bfloat16
F32 = jnp.float32


def dot_nn(left, right):
    return lax.dot_general(left, right, (((1,), (0,)), ((), ())), preferred_element_type=F32)


def dot_nt(left, right):
    return lax.dot_general(left, right, (((1,), (1,)), ((), ())), preferred_element_type=F32)


def dot_tn(left, right):
    return lax.dot_general(left, right, (((0,), (0,)), ((), ())), preferred_element_type=F32)


def params(mib, steps=1):
    return pltpu.CompilerParams(
        dimension_semantics=("arbitrary",) * steps, vmem_limit_bytes=mib << 20
    )


def cost(micros):
    return pl.CostEstimate(flops=int(micros * 1.1e8), transcendentals=0, bytes_accessed=0)


def whole(shape, at=0):
    zeros = (0,) * (len(shape) - 1)
    return pl.BlockSpec(shape, lambda *_: (at,) + zeros, pipeline_mode=pl.Buffered(1))


def image_spec(width):
    return pl.BlockSpec((1, SEQ, width), lambda i, *_: (i, 0, 0))


def resident(shape):
    zeros = (0,) * len(shape)
    return pl.BlockSpec(shape, lambda *_: zeros)


def placed(operands, keep=()):
    return [
        item
        if any(item is kept for kept in keep)
        else pltpu.with_memory_space_constraint(item, pltpu.HBM)
        for item in operands
    ]


def in_hbm(shape, dtype):
    return pltpu.HBM(tuple(shape), dtype)


def shaped(shape, dtype):
    return jax.ShapeDtypeStruct(shape, dtype)


TILE = 40


def normalise(values):
    mean = jnp.mean(values, axis=-1, keepdims=True)
    centred = values - mean
    spread = jnp.mean(centred * centred, axis=-1, keepdims=True)
    scale = lax.rsqrt(spread + 1e-06)
    return centred * scale, scale


def normalise_back(grad, gain, xhat, scale):
    u = grad * gain
    return (
        u - jnp.mean(u, axis=-1, keepdims=True) - xhat * jnp.mean(u * xhat, axis=-1, keepdims=True)
    ) * scale


def line(ref):
    return ref[...].reshape(1, -1)


def token_line(ids_ref, token_ref):
    tokens = token_ref[...].astype(F32)
    group = lax.broadcasted_iota(jnp.int32, tokens.shape, 0)
    return jnp.sum(jnp.where(group == ids_ref[pl.program_id(0)], tokens, 0.0), axis=0, keepdims=True)


def mixed(patch_ref, sel_ref, token, at):
    sel = sel_ref[0, at : at + TILE, :]
    return patch_ref[0, at : at + TILE, :].astype(F32) * (1.0 - sel) + sel * token, sel


def tiles():
    return range(0, SEQ, TILE)


def fold(values):
    return jnp.sum(values.reshape(values.shape[0] // 8, 8, values.shape[1]), axis=0)


SMALL_ROWS = 16


def prepare_kernel(
    side_ref, qkv_ref, out_ref, down_ref, qb_ref, vb_ref, upb_ref, table_ref,
    small_ref, attn_ref, half_ref, pack_ref,
):
    own = qb_ref.shape[0]
    width = small_ref.shape[1]
    small_ref[...] = jnp.zeros_like(small_ref)
    small_ref[0:1, :own] = line(qb_ref)
    small_ref[0:1, 2 * own : 3 * own] = line(vb_ref)
    small_ref[1:2, : upb_ref.shape[0]] = line(upb_ref)
    small_ref[2 : 2 + table_ref.shape[0], : table_ref.shape[1]] = table_ref[...]
    attn_ref[2 * own :, :] = small_ref[...]
    pack_ref[: 3 * own, :] = qkv_ref[...]
    pack_ref[3 * own :, :] = out_ref[...]

    @pl.when(side_ref[0] == 0)
    def _():
        attn_ref[: 2 * own, :] = qkv_ref[: 2 * own, :]
        half_ref[...] = down_ref[:, : width // 2]

    @pl.when(side_ref[0] == 1)
    def _():
        attn_ref[:own, :] = qkv_ref[2 * own :, :]
        attn_ref[own : 2 * own, :] = out_ref[...]
        half_ref[...] = down_ref[:, width // 2 :]


def prepare(side, qkv, out, down, qb, vb, upb, table):
    width = out.shape[1]
    vmem = pl.BlockSpec(memory_space=pltpu.VMEM)
    return pl.pallas_call(
        prepare_kernel,
        out_shape=[
            shaped((SMALL_ROWS, width), BF),
            shaped((2 * qb.shape[0] + SMALL_ROWS, width), BF),
            shaped((down.shape[0], width // 2), BF),
            shaped((4 * qb.shape[0], width), BF),
        ],
        in_specs=[pl.BlockSpec(memory_space=pltpu.SMEM)] + [vmem] * 7,
        out_specs=[vmem] * 4,
        compiler_params=params(8, 0),
        cost_estimate=cost(2),
        name="prepare",
    )(side, *placed([qkv, out, down, qb, vb, upb, table]))


def bias_kernel(near_ref, far_ref, narrow_ref, out_ref, index_ref):
    own = out_ref.shape[0] // 2
    chunks = near_ref.shape[1] // LANES
    tables = (near_ref[...].astype(F32), far_ref[...].astype(F32))
    index_ref[...] = jnp.zeros_like(index_ref)
    index_ref[:, : narrow_ref.shape[1]] = narrow_ref[...]

    def rows_of(step, _):
        row = pl.multiple_of(step * 8, 8)
        for col in range(0, index_ref.shape[1], LANES):
            index = index_ref[pl.ds(row, 8), col : col + LANES]
            low = index & (LANES - 1)
            high = index >> 7
            for head in range(2 * own):
                table, at = tables[head // own], 2 + head % own
                found = jnp.zeros((8, LANES), F32)
                for chunk in range(chunks):
                    source = jnp.broadcast_to(
                        table[at : at + 1, chunk * LANES : (chunk + 1) * LANES], (8, LANES)
                    )
                    picked = jnp.take_along_axis(source, low, axis=1)
                    found = jnp.where(high == chunk, picked, found)
                out_ref[head, pl.ds(row, 8), col : col + LANES] = found
        return 0

    lax.fori_loop(0, SEQ // 8, rows_of, 0, unroll=5)


def small_spec(small):
    return whole((SMALL_ROWS, small[0].shape[1]), small[1])


def position_bias(small, heads, index):
    return pl.pallas_call(
        bias_kernel,
        out_shape=shaped((heads, SEQ, 2 * LANES), F32),
        grid=(1,),
        in_specs=[small_spec(item) for item in small] + [whole(index.shape)],
        out_specs=resident((heads, SEQ, 2 * LANES)),
        scratch_shapes=[pltpu.VMEM((SEQ, 2 * LANES), jnp.int32)],
        compiler_params=params(6),
        cost_estimate=cost(2),
        name="position_bias",
    )(*placed([item for item, _ in small] + [index]))


TABLE_ROWS = 8


def table_kernel(*refs):
    total_refs, (index_ref, out_ref) = refs[:-2], refs[-2:]

    @pl.when(pl.program_id(0) == 0)
    def _():
        out_ref[...] = jnp.zeros_like(out_ref)

    chunks = out_ref.shape[0] // sum(ref.shape[0] for ref in total_refs)
    spots = lax.broadcasted_iota(jnp.int32, (LANES, SEQ), 0)
    acc = jnp.zeros(out_ref.shape, F32)
    for row in range(TABLE_ROWS):
        index = index_ref[row : row + 1, :]
        hot = (spots == (index & (LANES - 1))).astype(F32).astype(BF)
        high = index >> 7
        total = jnp.concatenate([ref[:, row, :] for ref in total_refs], axis=0)
        parts = [jnp.where(high == chunk, total, 0.0) for chunk in range(chunks)]
        acc = acc + dot_nt(jnp.concatenate(parts, axis=0).astype(BF), hot)
    out_ref[...] += acc


def table_sums(totals, index, chunks, first, steps):
    own = totals[0][0].shape[0]
    heads = own * len(totals)
    return pl.pallas_call(
        table_kernel,
        out_shape=shaped((chunks * heads, LANES), F32),
        grid=(steps,),
        in_specs=[
            pl.BlockSpec((own, TABLE_ROWS, SEQ), lambda i, at=at: (at, first + i, 0))
            for _, at in totals
        ]
        + [pl.BlockSpec((TABLE_ROWS, SEQ), lambda i: (first + i, 0))],
        out_specs=resident((chunks * heads, LANES)),
        compiler_params=params(6),
        cost_estimate=cost(5),
        name="table_sums",
    )(*placed([total for total, _ in totals] + [index]))


def block(values, at):
    return values[:, at * LANES : (at + 1) * LANES]


def turned(values):
    return pltpu.roll(values, HEAD, 1)


def only(keep, values):
    return jnp.where(keep, values, jnp.zeros_like(values))


def lower_lanes():
    return lax.broadcasted_iota(jnp.int32, (SEQ, LANES), 1) < HEAD


def shard_forward(x, weight_ref, small_ref, bias_ref, mask, joint_ref, probs_ref, context_ref, base):
    width = joint_ref.shape[2]
    own = width // 3
    low = lower_lanes()
    high = jnp.logical_not(low)
    column = lax.broadcasted_iota(jnp.int32, (1, width), 1)
    scale = jnp.where(column < own, HEAD**-0.5, 1.0)
    joint = dot_nt(x, weight_ref[...])
    joint_ref[0] = ((joint + small_ref[...].astype(F32)[0:1, :width]) * scale).astype(BF)
    joint = joint_ref[0]
    b1, b2, b3 = block(joint, 1), block(joint, 2), block(joint, 3)
    t0, t1 = turned(block(joint, 0)), turned(b1)
    left = [only(high, b1), only(low, b2), only(high, b2)]
    right = [t0, t0, t1]
    value = [b3, b3, joint[:, 4 * LANES :]]
    heads = range(3)
    scores = [dot_nt(left[i], right[i]) + bias_ref[base + i][:, :SEQ] + mask for i in heads]
    raised = [jnp.exp(item - jnp.max(item, axis=0, keepdims=True)) for item in scores]
    probs = [(item * (1.0 / jnp.sum(item, axis=0, keepdims=True))).astype(BF) for item in raised]
    for i in heads:
        probs_ref[0, base + i] = probs[i]
    found = [dot_tn(probs[i], value[i]) for i in heads]
    context_ref[0, :, :LANES] = jnp.where(low, found[0], found[1]).astype(BF)
    context_ref[0, :, LANES:] = found[2].astype(BF)


def attend_kernel(first, last, parted, *refs):
    refs = list(refs)

    def take(count):
        found = refs[:count]
        del refs[:count]
        return found

    if first or last:
        (ids_ref,) = take(1)
    if parted:
        (side_ref,) = take(1)
    if first or last:
        patch_ref, sel_ref, token_ref, gain_ref, shift_ref = take(5)
    if last:
        obias_ref, gamma_ref = take(2)
    if not first:
        x_ref, part_in_ref = take(2)
    weight_ref, out_ref, small_ref, bias_ref, mask_ref = take(5)
    if first:
        (x_ref,) = take(1)
    joint_ref, probs_ref, context_ref, part_ref = take(4)
    if last:
        middle_ref, normed_ref = take(2)
    if parted:
        p_ref, q_ref = weight_ref, out_ref
        (pack_ref,) = take(1)
        half = p_ref.shape[0] - SMALL_ROWS

        @pl.when(pl.program_id(0) == 0)
        def _():
            for side in range(2):
                @pl.when(side_ref[0] == side)
                def _():
                    pack_ref[side * half : (side + 1) * half, :] = p_ref[:half, :]
                    pack_ref[(1 - side) * half : (2 - side) * half, :] = q_ref[:half, :]

        joint = joint_ref.shape[2]
        weight_ref, out_ref = pack_ref.at[:joint], pack_ref.at[joint:]
    if first:
        token = token_line(ids_ref, token_ref)
        for at in tiles():
            start, _ = mixed(patch_ref, sel_ref, token, at)
            xhat, _ = normalise(start)
            x_ref[0, at : at + TILE, :] = (xhat * line(gain_ref) + line(shift_ref)).astype(BF)
    shard_forward(
        x_ref[0], weight_ref, small_ref, bias_ref, mask_ref[0], joint_ref, probs_ref, context_ref, 0
    )
    part = dot_nn(context_ref[0], out_ref[...])
    part_ref[0] = part if first else part + part_in_ref[0]
    if last:
        token = token_line(ids_ref, token_ref)
        for at in tiles():
            rows = slice(at, at + TILE)
            start, _ = mixed(patch_ref, sel_ref, token, at)
            value = part_ref[0, rows, :] + line(obias_ref)
            middle = start + line(gamma_ref) * value
            xhat, _ = normalise(middle)
            part_ref[0, rows, :] = value
            middle_ref[0, rows, :] = middle
            normed_ref[0, rows, :] = (xhat * line(gain_ref) + line(shift_ref)).astype(BF)


def mix_specs(width, groups):
    return [
        image_spec(width),
        pl.BlockSpec((1, SEQ, 1), lambda i, ids, *_: (ids[i], 0, 0)),
        whole((groups, width)),
    ]


def attend(mix, norm, weight, out, small, bias, turn, mask, x=None, part=None, side=None, after=None):
    ids, patches, sel_table, tokens = mix
    images, _, width = patches.shape
    heads = bias.shape[0] // 2
    own = heads * HEAD
    first, last, parted = x is None, after is not None, side is not None
    prefetch, in_specs, operands = [], [], []
    if first or last:
        prefetch.append(ids)
    if parted:
        prefetch.append(side)
    if first or last:
        in_specs += mix_specs(width, tokens.shape[0]) + [whole((width,))] * 2
        operands += [patches, sel_table, tokens, *norm]
    if last:
        in_specs += [whole((width,))] * 2
        operands += list(after)
    if not first:
        in_specs += [image_spec(width)] * 2
        operands += [x, part]
    if parted:
        in_specs += [whole(weight.shape), whole(out.shape)]
    else:
        in_specs += [whole((3 * own, width)), whole((own, width), out[1])]
        out = out[0]
    in_specs += [small_spec(small)]
    in_specs += [whole((heads,) + bias.shape[1:], turn), image_spec(1)]
    operands += [weight, out, small[0], bias, mask]
    outs = [
        (in_hbm((images, SEQ, 3 * own), BF), image_spec(3 * own)),
        (
            in_hbm((images, heads, SEQ, SEQ), BF),
            pl.BlockSpec((1, heads, SEQ, SEQ), lambda i, *_: (i, 0, 0, 0)),
        ),
        (in_hbm((images, SEQ, own), BF), image_spec(own)),
        (shaped(patches.shape, F32), image_spec(width)),
    ]
    if first:
        outs = [(in_hbm(patches.shape, BF), image_spec(width))] + outs
    if last:
        outs += [
            (shaped(patches.shape, F32), image_spec(width)),
            (shaped(patches.shape, BF), image_spec(width)),
        ]
    if parted:
        outs.append((in_hbm((4 * own, width), BF), resident((4 * own, width))))
    return pl.pallas_call(
        functools.partial(attend_kernel, first, last, parted),
        out_shape=[shape for shape, _ in outs],
        grid_spec=pltpu.PrefetchScalarGridSpec(
            num_scalar_prefetch=len(prefetch),
            grid=(images,),
            in_specs=in_specs,
            out_specs=[spec for _, spec in outs],
        ),
        compiler_params=params(14),
        cost_estimate=cost(9),
        name="attend",
    )(*prefetch, *placed(operands, [part, bias]))


def shards_backward(x, grad, shards, total_ref):
    low = lower_lanes()
    high = jnp.logical_not(low)
    left, right, queries, keys, probs = [], [], [], [], []
    for joint_ref, probs_ref, _, _, out_ref, _, _, _ in shards:
        grad_context = dot_nt(grad, out_ref[...]).astype(BF)
        d0, d1 = grad_context[:, :LANES], grad_context[:, LANES:]
        joint = joint_ref[0]
        b3 = block(joint, 3)
        t0, t1, t2 = turned(block(joint, 0)), turned(block(joint, 1)), turned(block(joint, 2))
        left += [only(low, b3), only(high, b3), joint[:, 4 * LANES :]]
        right += [d0, d0, d1]
        queries += [t0, t0, t1]
        keys += [t1, t2, t2]
        probs += [probs_ref[0, i] for i in range(3)]
    heads = range(len(left))
    grad_probs = [dot_nt(left[i], right[i]) for i in heads]
    grads_v = [dot_nn(probs[i], right[i]) for i in heads]
    grad_scores = []
    for i in heads:
        wide = probs[i].astype(F32)
        centre = jnp.sum(wide * grad_probs[i], axis=0, keepdims=True)
        grad_scores.append((wide * (grad_probs[i] - centre)).astype(BF))
    for i in heads:
        total_ref[i] += grad_scores[i].astype(F32)
    grads_k = [dot_nn(grad_scores[i], queries[i]) for i in heads]
    grads_q = [dot_tn(grad_scores[i], keys[i]) for i in heads]
    scale = HEAD**-0.5
    part = None
    for which, (_, _, context_ref, weight_ref, _, sums_ref, acc_ref, joint_grad_ref) in enumerate(shards):
        gq, gk, gv = (items[3 * which : 3 * which + 3] for items in (grads_q, grads_k, grads_v))
        blocks = [
            jnp.where(low, gq[0], gq[1]) * scale,
            jnp.where(low, gq[2] * scale, gk[0]),
            jnp.where(low, gk[1], gk[2]),
            jnp.where(low, gv[0], gv[1]),
            gv[2],
        ]
        for at, values in enumerate(blocks):
            cols = slice(at * LANES, at * LANES + values.shape[1])
            held = values.astype(BF)
            joint_grad_ref[:, cols] = held
            sums_ref[:, cols] += fold(held.astype(F32))
        width = joint_grad_ref.shape[1]
        joint_grad = joint_grad_ref[...]
        acc_ref[:width, :] += dot_tn(joint_grad, x)
        acc_ref[width:, :] += dot_tn(context_ref[0], grad)
        own = dot_nn(joint_grad, weight_ref[...])
        part = own if part is None else part + own
    return part


def attend_back_kernel(first, last, count, *refs):
    refs = list(refs)

    def take(number):
        found = refs[:number]
        del refs[:number]
        return found

    (ids_ref,) = take(1)
    if last:
        patch_ref, sel_ref, token_ref, gmiddle_ref, gain_ref = take(5)
    if not first:
        (carried_ref,) = take(1)
    x_ref, grad_ref = take(2)
    inputs = [take(5) for _ in range(count)]
    outputs = [take(2) for _ in range(count)]
    (total_ref,) = take(1)
    if last:
        patch_out_ref, norm_ref, token_out_ref = take(3)
    else:
        (carry_out_ref,) = take(1)
    scratch = [take(2) for _ in range(count)]
    step = pl.program_id(0)

    @pl.when(step == 0)
    def _():
        zeroed = [total_ref] + [item[1] for item in outputs] + [item[0] for item in scratch]
        for ref in zeroed + ([norm_ref] if last else []):
            ref[...] = jnp.zeros_like(ref)

    shards = [
        (*ins, out[1], own[0], own[1]) for ins, out, own in zip(inputs, outputs, scratch)
    ]
    part = shards_backward(x_ref[0], grad_ref[0], shards, total_ref)
    if not first:
        part = part + carried_ref[0]
    if last:
        (carry_ref,) = refs
        carry_ref[...] = part
        token = token_line(ids_ref, token_ref)
        token_sum = jnp.zeros((8, part.shape[1]), F32)
        for at in tiles():
            rows = slice(at, at + TILE)
            start, sel = mixed(patch_ref, sel_ref, token, at)
            xhat, scale = normalise(start)
            grad_normed = carry_ref[rows, :]
            norm_ref[0:8, :] += fold(grad_normed * xhat)
            norm_ref[8:16, :] += fold(grad_normed)
            grad_start = gmiddle_ref[0, rows, :] + normalise_back(
                grad_normed, line(gain_ref), xhat, scale
            )
            patch_out_ref[0, rows, :] = grad_start * (1.0 - sel)
            token_sum = token_sum + fold(grad_start * sel)
        token_out_ref[0] = token_sum
    else:
        carry_out_ref[0] = part

    @pl.when(step == pl.num_programs(0) - 1)
    def _():
        for out, own in zip(outputs, scratch):
            out[0][...] = own[0][...].astype(BF)


def attend_back(ids, x, grad, shards, carried, tail):
    images, _, width = x.shape
    joint_width = shards[0][0].shape[2]
    own = joint_width // 3
    heads = own // HEAD
    count = len(shards)
    square = pl.BlockSpec((1, heads, SEQ, SEQ), lambda i, *_: (i, 0, 0, 0))
    first, last = carried is None, tail is not None
    in_specs = [image_spec(width)] * 2
    operands = [x, grad]
    for joint, probs, context, weight, weight_at, out, out_at in shards:
        in_specs += [image_spec(joint_width), square, image_spec(own)]
        in_specs += [whole((joint_width, width), weight_at), whole((own, width), out_at)]
        operands += [joint, probs, context, weight, out]
    if not first:
        in_specs = [image_spec(width)] + in_specs
        operands = [carried] + operands
    out_shape, out_specs, scratch = [], [], []
    for _ in shards:
        out_shape += [in_hbm((joint_width + own, width), BF), in_hbm((8, joint_width), F32)]
        out_specs += [resident((joint_width + own, width)), resident((8, joint_width))]
        scratch += [pltpu.VMEM((joint_width + own, width), F32), pltpu.VMEM((SEQ, joint_width), BF)]
    out_shape.append(in_hbm((count * heads, SEQ, SEQ), F32))
    out_specs.append(resident((count * heads, SEQ, SEQ)))
    if last:
        patches, sel_table, tokens, grad_middle, gain = tail
        in_specs = (
            mix_specs(width, tokens.shape[0]) + [image_spec(width), whole((width,))] + in_specs
        )
        operands = [patches, sel_table, tokens, grad_middle, gain] + operands
        out_shape += [
            shaped(x.shape, F32), shaped((16, width), F32), shaped((images, 8, width), F32)
        ]
        out_specs += [
            image_spec(width),
            resident((16, width)),
            pl.BlockSpec((1, 8, width), lambda i, *_: (i, 0, 0)),
        ]
        scratch.append(pltpu.VMEM((SEQ, width), F32))
    else:
        out_shape.append(in_hbm(x.shape, F32))
        out_specs.append(image_spec(width))
    return pl.pallas_call(
        functools.partial(attend_back_kernel, first, last, count),
        out_shape=out_shape,
        grid_spec=pltpu.PrefetchScalarGridSpec(
            num_scalar_prefetch=1,
            grid=(images,),
            in_specs=in_specs,
            out_specs=out_specs,
            scratch_shapes=scratch,
        ),
        compiler_params=params(14 if count == 1 else 24),
        cost_estimate=cost(13 * count),
        name="attend_back",
    )(ids, *placed(operands))


MLP_MIB = 40


def mlp_kernel(first, lengths, *refs):
    refs = list(refs)

    def take(number):
        found = refs[:number]
        del refs[:number]
        return found

    count = len(lengths)
    (side_ref,) = take(1)
    x_ref, cot_ref, gamma_ref = take(3)
    shards = [take(length) for length in lengths]
    if not first:
        carried = take(2)
    totals = take(2)
    grads = take(count)
    upb_grad_ref, gm_ref, up_ref, down_ref, held_ref, value_ref, grad_ref, in_sem, out_sem, sem = refs
    accs = (value_ref, grad_ref)
    step = pl.program_id(0)

    def moves(sources, targets, sems):
        return [
            pltpu.make_async_copy(source, target, sems.at[at])
            for at, (source, target) in enumerate(zip(sources, targets))
        ]

    def weights(at):
        shard = shards[at]
        if len(shard) == 3:
            targets = [up_ref.at[at], down_ref.at[at]]
        else:
            half = shard[1].shape[1]
            places = [
                pl.ds(pl.multiple_of(place * half, LANES), half)
                for place in (side_ref[0], 1 - side_ref[0])
            ]
            targets = [up_ref.at[at]] + [down_ref.at[at, :, place] for place in places]
        return moves(shard[:-1], targets, in_sem.at[at])

    @pl.when(step == 0)
    def _():
        for at in range(count):
            for move in weights(at):
                move.start()
        if first:
            for ref in accs:
                ref[...] = jnp.zeros_like(ref)
        else:
            for move in moves(carried, accs, sem):
                move.start()
        gm_ref[...] = (line(gamma_ref) * cot_ref[...].astype(F32)).astype(BF)

    for at in range(count):
        @pl.when(step == at)
        def _():
            for move in weights(at):
                move.wait()

    x = x_ref[...]
    gm = gm_ref[...]
    up = up_ref[step]
    down = down_ref[step]
    upb = shards[0][-1][...].astype(F32)[1:2, :]
    for at in range(1, count):
        upb = jnp.where(step == at, shards[at][-1][...].astype(F32)[1:2, :], upb)
    before = dot_nn(x, up) + upb
    share = 0.5 + 0.5 * lax.erf(before * (0.5**0.5))
    density = jnp.exp(before * before * -0.5) * ((2.0 * jnp.pi) ** -0.5)
    hidden = (before * share).astype(BF)
    slope = share + before * density
    grad_before = (dot_nt(gm, down) * slope).astype(BF)
    upb_grad_ref[...] = fold(grad_before.astype(F32))
    held_ref[step, x.shape[1] :, :] = dot_tn(hidden, gm).astype(BF)
    held_ref[step, : x.shape[1], :] = dot_tn(x, grad_before).astype(BF)
    for at in range(count):
        @pl.when(step == at)
        def _():
            pltpu.make_async_copy(held_ref.at[at], grads[at], out_sem.at[at]).start()

    if not first:
        @pl.when(step == 0)
        def _():
            for move in moves(carried, accs, sem):
                move.wait()

    value_ref[...] += dot_nn(hidden, down)
    grad_ref[...] += dot_nt(grad_before, up)

    @pl.when(step == count - 1)
    def _():
        for move in moves(accs, totals, sem):
            move.start()
        for move in moves(accs, totals, sem):
            move.wait()
        for at in range(count):
            pltpu.make_async_copy(held_ref.at[at], grads[at], out_sem.at[at]).wait()


def mlp(x, cot, gamma, shards, carried, side):
    rows, width = x.shape
    hidden = shards[0][0].shape[1]
    first = carried is None
    count = len(shards)
    anywhere = pl.BlockSpec(memory_space=pl.ANY)
    in_specs = [whole((rows, width)), whole((rows, width)), whole((width,))]
    operands = [x, cot, gamma]
    for shard in shards:
        in_specs += [anywhere] * (len(shard) - 1) + [small_spec(shard[-1])]
        operands += list(shard[:-1]) + [shard[-1][0]]
    aliases = {}
    if not first:
        at = len(operands) + 1
        aliases = {at: 0, at + 1: 1}
        in_specs += [anywhere] * 2
        operands += list(carried)
    total = shaped((rows, width), F32)
    grads = [in_hbm((width + hidden, width), BF)]
    grad_specs = [anywhere]
    return pl.pallas_call(
        functools.partial(mlp_kernel, first, [len(shard) for shard in shards]),
        out_shape=[total, total] + grads * count + [shaped((8 * count, hidden), F32)],
        grid_spec=pltpu.PrefetchScalarGridSpec(
            num_scalar_prefetch=1,
            grid=(count,),
            in_specs=in_specs,
            out_specs=[anywhere] * 2
            + grad_specs * count
            + [pl.BlockSpec((8, hidden), lambda i, *_: (i, 0))],
            scratch_shapes=[
                pltpu.VMEM((rows, width), BF),
                pltpu.VMEM((count, width, hidden), BF),
                pltpu.VMEM((count, hidden, width), BF),
                pltpu.VMEM((count, width + hidden, width), BF),
                pltpu.VMEM((rows, width), F32),
                pltpu.VMEM((rows, width), F32),
                pltpu.SemaphoreType.DMA((count, 3)),
                pltpu.SemaphoreType.DMA((count,)),
                pltpu.SemaphoreType.DMA((2,)),
            ],
        ),
        input_output_aliases=aliases,
        compiler_params=params(MLP_MIB),
        cost_estimate=cost(9 * count),
        name="mlp",
    )(side, *placed(operands, [x] + list(carried or [])))


def middle_back_kernel(
    value_ref, grad_ref, middle_ref, attn_ref, cot_ref, dbias_ref, gmlp_ref, gattn_ref, gain_ref,
    out_ref, gmiddle_ref, gattn_out_ref, sums_ref,
):
    @pl.when(pl.program_id(0) == 0)
    def _():
        sums_ref[...] = jnp.zeros_like(sums_ref)

    def add(row, values):
        sums_ref[8 * row : 8 * row + 8, :] += fold(values)

    for at in tiles():
        rows = slice(at, at + TILE)
        value = value_ref[0, rows, :] + line(dbias_ref)
        cot = cot_ref[0, rows, :].astype(F32)
        middle = middle_ref[0, rows, :]
        out_ref[0, rows, :] = (middle + line(gmlp_ref) * value).astype(BF)
        add(0, cot * value)
        add(1, (line(gmlp_ref) * cot).astype(BF).astype(F32))
        xhat, scale = normalise(middle)
        grad = grad_ref[0, rows, :]
        add(2, grad * xhat)
        add(3, grad)
        grad_middle = cot + normalise_back(grad, line(gain_ref), xhat, scale)
        gmiddle_ref[0, rows, :] = grad_middle
        add(4, grad_middle * attn_ref[0, rows, :])
        grad_attn = (line(gattn_ref) * grad_middle).astype(BF)
        gattn_out_ref[0, rows, :] = grad_attn
        add(5, grad_attn.astype(F32))


def middle_back(value, grad, middle, attn, cot, vectors):
    images, _, width = middle.shape
    return pl.pallas_call(
        middle_back_kernel,
        out_shape=(
            in_hbm(middle.shape, BF),
            in_hbm(middle.shape, F32),
            in_hbm(middle.shape, BF),
            shaped((48, width), F32),
        ),
        grid=(images,),
        in_specs=[image_spec(width)] * 5 + [whole((width,))] * 4,
        out_specs=(image_spec(width),) * 3 + (resident((48, width)),),
        compiler_params=params(12),
        cost_estimate=cost(5),
        name="middle_back",
    )(*placed([value, grad, middle, attn, cot, *vectors], [value, grad, middle, attn]))


def swap(values, axis, mask):
    count = lax.axis_size(axis)
    return lax.ppermute(values, axis, [(i, i ^ mask) for i in range(count)])


def dp_masks():
    count = lax.axis_size("dp")
    return [1 << bit for bit in range(count.bit_length() - 1)]


def pinned(value, *others):
    return lax.optimization_barrier((value,) + others)[0]


def plus(left, right):
    return (left.astype(F32) + right.astype(F32)).astype(BF)


ORDERS = ((0, 1), (1, 2))


def axis_bits():
    place = lax.axis_index("dp")
    return jnp.stack([(place >> bit) & 1 for bit in range(len(dp_masks()))]).astype(jnp.int32)


def halves_of(ref, base, size, bit):
    keep = pl.multiple_of(base + bit * size, 16)
    sent = pl.multiple_of(base + (1 - bit) * size, 16)
    return ref[pl.ds(keep, size), :], ref[pl.ds(sent, size), :]


def split_kernel(bits_ref, a_ref, b_ref, c_ref, *refs):
    outs, total_ref = refs[:4], refs[4]
    for at in range(0, total_ref.shape[0], 64):
        rows = slice(at, at + 64)
        total_ref[rows, :] = (
            a_ref[rows, :].astype(F32) + b_ref[rows, :].astype(F32) + c_ref[rows, :].astype(F32)
        ).astype(BF)
    part = total_ref.shape[0] // 2
    for which in range(2):
        keep, sent = halves_of(total_ref, which * part, part // 2, bits_ref[ORDERS[which][0]])
        outs[2 * which][...] = keep
        outs[2 * which + 1][...] = sent


def again_kernel(bits_ref, *refs):
    ins, outs, totals = refs[:4], refs[4:8], refs[8:]
    for which in range(2):
        total_ref = totals[which]
        total_ref[...] = plus(ins[2 * which][...], ins[2 * which + 1][...])
        size = total_ref.shape[0] // 2
        keep, sent = halves_of(total_ref, 0, size, bits_ref[ORDERS[which][1]])
        outs[2 * which][...] = keep
        outs[2 * which + 1][...] = sent


def both_kernel(bits_ref, *refs):
    for which in range(2):
        refs[4 + which][...] = plus(refs[2 * which][...], refs[2 * which + 1][...])


def put(out_ref, base, own, other, bit):
    size = own.shape[0]
    out_ref[pl.ds(pl.multiple_of(base + bit * size, 16), size), :] = own.astype(out_ref.dtype)
    out_ref[pl.ds(pl.multiple_of(base + (1 - bit) * size, 16), size), :] = other.astype(out_ref.dtype)


def grow_kernel(bits_ref, *refs):
    for which in range(2):
        put(refs[4 + which], 0, refs[2 * which][...], refs[2 * which + 1][...], bits_ref[ORDERS[which][1]])


def whole_kernel(bits_ref, *refs):
    ins, (*out_refs, total_ref) = refs[:4], refs[4:]
    part = total_ref.shape[0] // 2
    for which in range(2):
        put(total_ref, which * part, ins[2 * which][...], ins[2 * which + 1][...], bits_ref[ORDERS[which][0]])
    base = 0
    for out_ref in out_refs:
        out_ref[...] = total_ref[base : base + out_ref.shape[0], :].astype(F32)
        base += out_ref.shape[0]


def step_call(kernel, bits, arrays, outs, scratch, name):
    vmem = pl.BlockSpec(memory_space=pltpu.VMEM)
    return pl.pallas_call(
        kernel,
        out_shape=outs,
        in_specs=[pl.BlockSpec(memory_space=pltpu.SMEM)] + [vmem] * len(arrays),
        out_specs=[vmem] * len(outs),
        scratch_shapes=scratch,
        compiler_params=params(12, 0),
        cost_estimate=cost(1),
        name=name,
    )(bits, *arrays)


def dp_chain(pieces, sizes):
    bits = axis_bits()
    masks = dp_masks()
    rows, width = pieces[0].shape
    quarter, eighth = shaped((rows // 4, width), BF), shaped((rows // 8, width), BF)
    rest = [[axis for axis in range(len(masks)) if axis not in order] for order in ORDERS]

    def send(a, b, axes):
        return [swap(array, "dp", masks[axis]) for array, axis in zip((a, b), axes)]

    a, a_sent, b, b_sent = step_call(
        split_kernel, bits, placed(pieces), [quarter] * 4, [pltpu.VMEM((rows, width), BF)], "dp_split"
    )
    a_got, b_got = yield send(a_sent, b_sent, [ORDERS[0][0], ORDERS[1][0]])
    a, a_sent, b, b_sent = step_call(
        again_kernel, bits, [a, a_got, b, b_got], [eighth] * 4,
        [pltpu.VMEM((rows // 4, width), BF)] * 2, "dp_again",
    )
    a_got, b_got = yield send(a_sent, b_sent, [ORDERS[0][1], ORDERS[1][1]])
    a, b = step_call(both_kernel, bits, [a, a_got, b, b_got], [eighth] * 2, [], "dp_both")
    for axes in zip(*rest):
        a_got, b_got = yield send(a, b, axes)
        a, b = step_call(both_kernel, bits, [a, a_got, b, b_got], [eighth] * 2, [], "dp_both")
    a_got, b_got = yield send(a, b, [ORDERS[0][1], ORDERS[1][1]])
    a, b = step_call(grow_kernel, bits, [a, a_got, b, b_got], [quarter] * 2, [], "dp_grow")
    a_got, b_got = yield send(a, b, [ORDERS[0][0], ORDERS[1][0]])
    return step_call(
        whole_kernel, bits, [a, a_got, b, b_got],
        [shaped((size, width), F32) for size in sizes], [pltpu.VMEM((rows, width), BF)], "dp_whole",
    )


class Chain:
    def __init__(self, steps):
        self.steps = steps
        self.done = None
        self.got = next(self.steps)

    def go_on(self):
        try:
            self.got = self.steps.send(self.got)
        except StopIteration as stop:
            self.done, self.got = stop.value, []


def together(*chains):
    flat = list(lax.optimization_barrier(tuple(item for chain in chains for item in chain.got)))
    for chain in chains:
        chain.got, flat = flat[: len(chain.got)], flat[len(chain.got) :]


def small_chain(held, sent, keep, own_rows):
    (got,) = yield [swap(sent, "mp", 1)]
    held = held + got
    sent = jnp.concatenate([held[keep + own_rows :], held[own_rows : keep + own_rows]], axis=0)
    (got,) = yield [swap(sent, "mp", 2)]
    held = held[: keep + own_rows] + got
    masks = dp_masks()
    for shift in masks[:-1]:
        (got,) = yield [swap(held, "dp", shift)]
        held = held + got
    (got,) = yield [swap(held, "dp", masks[-1])]
    return held, got


def collect_kernel(ids_ref, sums2_ref, sums1_ref, tokens_ref, table0_ref, table1_ref, *refs):
    upb_refs, joint_refs, (out_ref, sent_ref) = refs[:2], refs[2:6], refs[6:]
    upb_lines = [upb_refs[1][8:16, :], upb_refs[1][0:8, :], upb_refs[0][8:16, :], upb_refs[0][0:8, :]]
    out_ref[...] = jnp.zeros_like(out_ref)
    sent_ref[...] = jnp.zeros_like(sent_ref)
    table = table0_ref[...] + table1_ref[...]

    def total(values):
        return jnp.sum(values, axis=0, keepdims=True)

    lines = [total(sums2_ref[8 * i : 8 * i + 8, :]) for i in range(6)]
    lines += [total(sums1_ref[8 * i : 8 * i + 8, :]) for i in range(2)]
    images = [total(tokens_ref[i]) for i in range(tokens_ref.shape[0])]
    for group in range(GROUPS):
        found = jnp.zeros_like(images[0])
        for at, values in enumerate(images):
            found = found + jnp.where(ids_ref[at] == group, values, 0.0)
        lines.append(found)
    for at, values in enumerate(lines):
        out_ref[8 + at : 9 + at, :] = values
        sent_ref[8 + at : 9 + at, :] = values
    hidden = upb_refs[0].shape[1]
    for which in range(4):
        ref = out_ref if which % 2 == 0 else sent_ref
        base = 0 if which < 2 else 24
        ref[base : base + 1, :hidden] = total(upb_lines[which])
        joint = total(joint_refs[which][...])
        ref[base + 1 : base + 2, : joint.shape[1]] = joint
        per = table.shape[0] // (out_ref.shape[1] // LANES)
        own = per // 4
        for chunk in range(out_ref.shape[1] // LANES):
            ref[base + 2 : base + 2 + own, chunk * LANES : (chunk + 1) * LANES] = table[
                chunk * per + which * own : chunk * per + (which + 1) * own, :
            ]


def collect(ids, sums2, sums1, tokens, tables, upbs, joints):
    width = sums2.shape[1]
    vmem = pl.BlockSpec(memory_space=pltpu.VMEM)
    return pl.pallas_call(
        collect_kernel,
        out_shape=(shaped((32, width), F32), shaped((32, width), F32)),
        in_specs=[pl.BlockSpec(memory_space=pltpu.SMEM)] + [vmem] * 11,
        out_specs=(vmem, vmem),
        cost_estimate=cost(1),
        name="collect",
    )(ids, *placed([sums2, sums1, tokens, *tables, *upbs, *joints], [sums1, tokens, *tables]))


def emit_kernel(held_ref, got_ref, *outs):
    own = outs[9].shape[0]
    value = held_ref[...] + got_ref[...]
    for at in range(8):
        outs[at][...] = value[8 + at : 9 + at, :].reshape(-1)
    outs[8][...] = value[16:24, :]
    outs[9][...] = value[1:2, :own].reshape(-1)
    outs[10][...] = value[1:2, 2 * own : 3 * own].reshape(-1)
    outs[11][...] = value[2 : 2 + outs[11].shape[0], : outs[11].shape[1]]
    outs[12][...] = value[0:1, : outs[12].shape[0]].reshape(-1)


def emit(held, got, own, table_shape, hidden):
    width = held.shape[1]
    return pl.pallas_call(
        emit_kernel,
        out_shape=[shaped((width,), F32)] * 8
        + [
            shaped((GROUPS, width), F32),
            shaped((own,), F32),
            shaped((own,), F32),
            shaped(table_shape, F32),
            shaped((hidden,), F32),
        ],
        cost_estimate=cost(1),
        name="emit",
    )(held, got)


def local(
    patches, dataset_id, patch_masks, mask_tokens, key_mask, bias_index, norm1_gain, norm1_shift,
    qkv_weight, query_bias, value_bias, bias_table, out_weight, out_bias, gamma_attn, norm2_gain,
    norm2_shift, up_weight, up_bias, down_weight, down_bias, gamma_mlp, cotangent,
):
    rows, width = patches.shape
    images = rows // SEQ
    place = lax.axis_index("mp")
    own = qkv_weight.shape[2]
    own_heads = own // HEAD
    table_rows = bias_table.shape[0]
    chunks = width // LANES
    hidden = up_weight.shape[1]

    ids = lax.dynamic_slice_in_dim(dataset_id, place * images, images, 0)
    keys_here = lax.dynamic_slice_in_dim(key_mask, place * images, images, 0)
    mask = jnp.where(keys_here > 0, 0.0, -1e30).astype(F32)[:, :, None]
    sel_table = patch_masks.astype(F32)[:, :, None]
    images3 = patches.reshape(images, SEQ, width)
    cot3 = cotangent.reshape(images, SEQ, width)
    index = bias_index.T
    mix = (ids, images3, sel_table, mask_tokens)

    parity = lax.axis_index("dp") & 1
    side = parity.reshape(1)
    qkv_own = qkv_weight.transpose(1, 2, 0).reshape(3 * own, width)
    small, attn_half, down_half, pack0 = prepare(
        side, qkv_own, out_weight, down_weight, query_bias, value_bias, up_bias, bias_table.T
    )
    small0, small1 = (small, 0), (swap(small, "mp", 1), 0)
    attn_p2 = swap(attn_half, "mp", 2)
    down_p2 = swap(down_half, "mp", 2)
    pack1 = swap(pack0, "mp", 1)
    bias_near = position_bias([small0, small1], 2 * own_heads, index)
    up2 = swap(pinned(up_weight, bias_near), "mp", 2)
    up1, down1 = swap(up_weight, "mp", 1), swap(down_weight, "mp", 1)

    norm1 = [norm1_gain, norm1_shift]
    x1, j0, probs0, c0, part = attend(
        mix, norm1, qkv_own, (out_weight, 0), small0, bias_near, 0, mask
    )
    part, attn_p2 = lax.optimization_barrier((part, attn_p2))
    attn_q2 = swap(attn_p2, "dp", 1)
    attn_p3 = swap(attn_p2, "mp", 1)
    small2, small3 = (attn_p2, 2 * own // SMALL_ROWS), (attn_p3, 2 * own // SMALL_ROWS)
    j1, probs1, c1, part = attend(mix, norm1, pack1, (pack1, 3), small1, bias_near, 1, mask, x1, part)
    part, attn_q2 = lax.optimization_barrier((part, attn_q2))
    attn_q3 = swap(attn_q2, "mp", 1)
    bias_far = position_bias([small2, small3], 2 * own_heads, index)
    j2, probs2, c2, part, pack2 = attend(
        mix, norm1, attn_p2, attn_q2, small2, bias_far, 0, mask, x1, part, side
    )
    part, down_p2 = lax.optimization_barrier((part, down_p2))
    down_q2 = swap(down_p2, "dp", 1)
    down_p3 = swap(down_p2, "mp", 1)
    j3, probs3, c3, attn_value, middle, normed2, pack3 = attend(
        mix, [norm2_gain, norm2_shift], attn_p3, attn_q3, small3, bias_far, 1, mask, x1, part, side,
        [out_bias, gamma_attn],
    )

    x2 = normed2.reshape(rows, width)
    x2, up2, down_q2 = lax.optimization_barrier((x2, up2, down_q2))
    up3 = swap(up2, "mp", 1)
    down_q3 = swap(down_q2, "mp", 1)
    value, grad2, m3, m2, upb32 = mlp(
        x2, cotangent, gamma_mlp, [(up3, down_p3, down_q3, small3), (up2, down_p2, down_q2, small2)],
        None, side,
    )
    mlp_far = plus(m2, swap(m3, "mp", 1))
    x2, mlp_far = lax.optimization_barrier((x2, mlp_far))
    mr2 = swap(mlp_far, "mp", 2)
    value, grad2, m1, m0, upb10 = mlp(
        x2, cotangent, gamma_mlp, [(up1, down1, small1), (up_weight, down_weight, small0)],
        (value, grad2), side,
    )

    shape3 = (images, SEQ, width)
    output, grad_middle, grad_attn, sums2 = middle_back(
        value.reshape(shape3), grad2.reshape(shape3), middle, attn_value, cot3,
        [down_bias, gamma_mlp, gamma_attn, norm2_gain],
    )

    mr1 = [swap(m1[:width], "mp", 1), swap(m1[width:], "mp", 1)]
    grad_attn, *mr1 = lax.optimization_barrier((grad_attn, *mr1))
    g1, js1, g3, js3, total13, carried = attend_back(
        ids, x1, grad_attn,
        [(j1, probs1, c1, pack1, 0, pack1, 3), (j3, probs3, c3, pack3, 0, pack3, 3)], None, None,
    )
    mlp_sum = [
        (own.astype(F32) + near.astype(F32) + far.astype(F32)).astype(BF)
        for own, near, far in zip((m0[:width], m0[width:]), mr1, (mr2[:width], mr2[width:]))
    ]
    carried, *mlp_sum = lax.optimization_barrier((carried, *mlp_sum))
    up_sum, down_sum = lax.psum(tuple(mlp_sum), "dp")
    r3 = swap(g3, "mp", 1)
    g2, js2, total2, carried = attend_back(
        ids, x1, grad_attn, [(j2, probs2, c2, pack2, 0, pack2, 3)], carried, None
    )
    far = plus(g2, r3)
    carried, far, g1 = lax.optimization_barrier((carried, far, g1))
    r1 = swap(g1, "mp", 1)
    r2 = swap(far, "mp", 2)
    g0, js0, total0, patch_grad, sums1, token_images = attend_back(
        ids, x1, grad_attn, [(j0, probs0, c0, qkv_own, 0, out_weight, 0)], carried,
        (images3, sel_table, mask_tokens, grad_middle, norm1_gain),
    )
    totals = [(total0, 0), (total13, 0), (total2, 0), (total13, 1)]
    blocks = SEQ // TABLE_ROWS
    table0 = table_sums(totals, index, chunks, 0, blocks // 2)
    g0, r1, r2, table0 = lax.optimization_barrier((g0, r1, r2, table0))
    tail = Chain(dp_chain([g0, r1, r2], [3 * own, own]))
    table1 = table_sums(totals, index, chunks, blocks // 2, blocks - blocks // 2)
    held, sent = collect(
        ids, sums2, sums1, token_images, [table0, table1], [upb32, upb10], [js0, js1, js2, js3]
    )
    tail.go_on()
    small = Chain(small_chain(held, sent, 16, 8))
    while tail.done is None or small.done is None:
        going = [chain for chain in (tail, small) if chain.done is None]
        together(*going)
        for chain in going:
            chain.go_on()
    qkv_sum, out_sum = tail.done
    up_sum, down_sum = up_sum.astype(F32), down_sum.astype(F32)
    (
        gamma_mlp_grad, down_bias_grad, gain2_grad, shift2_grad, gamma_attn_grad, out_bias_grad,
        gain1_grad, shift1_grad, token_grad, qb_grad, vb_grad, table_grad, upb_grad,
    ) = emit(*small.done, own, (own_heads, table_rows), hidden)

    return (
        output.reshape(rows, width),
        patch_grad.reshape(rows, width),
        token_grad,
        gain1_grad,
        shift1_grad,
        qkv_sum.reshape(3, own, width).transpose(2, 0, 1),
        qb_grad,
        vb_grad,
        table_grad.T,
        out_sum,
        out_bias_grad,
        gamma_attn_grad,
        gain2_grad,
        shift2_grad,
        up_sum,
        upb_grad,
        down_sum,
        down_bias_grad,
        gamma_mlp_grad,
    )


def solution(mesh):
    return jax.shard_map(
        local,
        mesh=mesh,
        in_specs=(
            P(("dp", "mp"), None), P("dp"), P(), P(), P("dp", None), P(), P(), P(),
            P(None, None, "mp"), P("mp"), P("mp"), P(None, "mp"), P("mp", None), P(), P(), P(), P(),
            P(None, "mp"), P("mp"), P("mp", None), P(), P(), P(("dp", "mp"), None),
        ),
        out_specs=(
            P(("dp", "mp"), None), P(("dp", "mp"), None), P(), P(), P(), P(None, None, "mp"),
            P("mp"), P("mp"), P(None, "mp"), P("mp", None), P(), P(), P(), P(), P(None, "mp"),
            P("mp"), P("mp", None), P(), P(),
        ),
        check_vma=False,
    )
```

profile of v0, /device:TPU:0, one launch (start us, length us, event | category | flops | bytes accessed | tf_op | source)
XLA Modules:
  0.0 317.2 jit_solution(3231557863722092736)
XLA Ops:
  16.9 3.4 %position_bias.2.refs_9_.refs_5_ = f32[6,200,256]{2,1,0:T(8,128)S(1)} custom-call(bf16[16,768]{1,0:T(8,128)(2,1)} %copy-done, bf16[16,768]{1,0:T(8,128)(2,1)} %copy-done.25, s32[200,200]{1,0:T(8,128)} %bitcast.35), custom_call_target="tpu_custom_call" | custom-call | flops 220000000 | tf_op jit(solution)/shard_map/position_bias/pallas_call | solution.py:194
  20.3 10.5 %attend.4 = (bf16[5,200,768]{2,1,0:T(8,128)(2,1)}, bf16[5,200,576]{2,1,0:T(8,128)(2,1)}, bf16[5,3,200,200]{3,2,1,0:T(8,128)(2,1)}, bf16[5,200,192]{2,1,0:T(8,128)(2,1)}, f32[5,200,768]{2,1,0:T(8,128)S(1)}) custom-call(s32[5]{0:T(128)S(1)} %dynamic_slice.6.refs_0_.ids_ref, bf16[5,200,768]{2,1,0:T(8,128)(2,1)} %bitcast.29, f32[8,200,1]{2,1,0:T(8,128)} %copy.50.refs_2_.refs_3_, ...), custom_call_target="tpu_custom_call" | custom-call | flops 990000000 | tf_op jit(solution)/shard_map/attend/pallas_call | solution.py:408
  34.5 8.5 %attend.5 = (bf16[5,200,576]{2,1,0:T(8,128)(2,1)}, bf16[5,3,200,200]{3,2,1,0:T(8,128)(2,1)}, bf16[5,200,192]{2,1,0:T(8,128)(2,1)}, f32[5,200,768]{2,1,0:T(8,128)S(1)}) custom-call(bf16[5,200,768]{2,1,0:T(8,128)(2,1)} %get-tuple-element.143.refs_0_.refs_1_.refs_9_.refs_2_.refs_7_, f32[5,200,768]{2,1,0:T(8,128)S(1)} %get-tuple-element.146.refs_1_, ...), custom_call_target="tpu_custom_call" | custom-call | flops 990000000 | tf_op jit(solution)/shard_map/attend/pallas_call | solution.py:408
  43.0 4.2 %collective-permute-done.3.refs_4_ = bf16[400,768]{1,0:T(8,128)(2,1)S(1)} collective-permute-done((bf16[400,768]{1,0:T(8,128)(2,1)}, bf16[400,768]{1,0:T(8,128)(2,1)S(1)}, u32[]{:S(2)}, u32[]{:S(2)}) %collective-permute-start.3) | collective-permute-done | bytes 614432 | tf_op jit(solution)/shard_map/ppermute | solution.py:798
  48.1 3.4 %position_bias.3.refs_6_.refs_14_ = f32[6,200,256]{2,1,0:T(8,128)S(1)} custom-call(bf16[400,768]{1,0:T(8,128)(2,1)} %collective-permute-done.1.near_ref.refs_3_.refs_5_.refs_11_, bf16[400,768]{1,0:T(8,128)(2,1)} %copy-done.9, s32[200,200]{1,0:T(8,128)} %bitcast.36), custom_call_target="tpu_custom_call" | custom-call | flops 220000000 | tf_op jit(solution)/shard_map/position_bias/pallas_call | solution.py:194
  51.5 9.1 %attend.6 = (bf16[5,200,576]{2,1,0:T(8,128)(2,1)}, bf16[5,3,200,200]{3,2,1,0:T(8,128)(2,1)}, bf16[5,200,192]{2,1,0:T(8,128)(2,1)}, f32[5,200,768]{2,1,0:T(8,128)S(1)}, bf16[768,768]{1,0:T(8,128)(2,1)}) custom-call(s32[1]{0:T(128)} %bitcast.side_ref.refs_0_.refs_1_, bf16[5,200,768]{2,1,0:T(8,128)(2,1)} %get-tuple-element.143.refs_0_.refs_1_.refs_9_.refs_2_.refs_7_, ...), custom_call_target="tpu_custom_call" | custom-call | flops 990000000 | tf_op jit(solution)/shard_map/attend/pallas_call | solution.py:408
  63.1 11.5 %attend.7 = (bf16[5,200,576]{2,1,0:T(8,128)(2,1)}, bf16[5,3,200,200]{3,2,1,0:T(8,128)(2,1)}, bf16[5,200,192]{2,1,0:T(8,128)(2,1)}, f32[5,200,768]{2,1,0:T(8,128)...) custom-call(s32[5]{0:T(128)S(1)} %dynamic_slice.6.refs_0_.ids_ref, ...), custom_call_target="tpu_custom_call" | custom-call | flops 990000000 | tf_op jit(solution)/shard_map/attend/pallas_call | solution.py:408
  77.0 3.1 collective-permute-done.10.refs_5_
  82.8 20.0 %mlp.2 = (f32[1000,768]{1,0:T(8,128)S(1)}, f32[1000,768]{1,0:T(8,128)S(1)}, bf16[1536,768]{1,0:T(8,128)(2,1)}, bf16[1536,768]{1,0:T(8,128)(2,1)}, f32[16,768]{1,0:T(8,128)S(1)}) custom-call(s32[1]{0:T(128)} %bitcast.side_ref.refs_0_.refs_1_, bf16[1000,768]{1,0:T(8,128)(2,1)S(1)} %bitcast.26, bf16[1000,768]{1,0:T(8,128)(2,1)} %refs_2_.3, f32[768]{0:T(1024)} %gmlp_ref.1, ...), custom_call_target="tpu_custom_call" | custom-call | flops 1980000000 | tf_op jit(solution)/shard_map/mlp/pallas_call | solution.py:717
  103.6 6.1 %collective-permute-done.12 = bf16[1536,768]{1,0:T(8,128)(2,1)S(1)} collective-permute-done((bf16[1536,768]{1,0:T(8,128)(2,1)}, bf16[1536,768]{1,0:T(8,128)(2,1)S(1)}, u32[]{:S(2)}, u32[]{:S(2)}) %collective-permute-start.12) | collective-permute-done | bytes 2359328 | tf_op jit(solution)/shard_map/ppermute | solution.py:798
  113.7 20.1 %mlp.3 = (f32[1000,768]{1,0:T(8,128)S(1)}, f32[1000,768]{1,0:T(8,128)S(1)}, bf16[1536,768]{1,0:T(8,128)(2,1)}, bf16[1536,768]{1,0:T(8,128)(2,1)}, f32[16,768]{1,0:T(8,128)S(1)}) custom-call(s32[1]{0:T(128)} %bitcast.side_ref.refs_0_.refs_1_, bf16[1000,768]{1,0:T(8,128)(2,1)S(1)} %bitcast.27, ...), custom_call_target="tpu_custom_call", output_to_operand_aliasing={{0}: (10, {}), {1}: (11, {})} | custom-call | flops 1980000000 | tf_op jit(solution)/shard_map/mlp/pallas_call | solution.py:717
  136.2 6.7 %middle_back.1 = (bf16[5,200,768]{2,1,0:T(8,128)(2,1)}, f32[5,200,768]{2,1,0:T(8,128)}, bf16[5,200,768]{2,1,0:T(8,128)(2,1)}, f32[48,768]{1,0:T(8,128)S(1)}) custom-call(f32[5,200,768]{2,1,0:T(8,128)S(1)} %bitcast.24, f32[5,200,768]{2,1,0:T(8,128)S(1)} %bitcast.25, f32[5,200,768]{2,1,0:T(8,128)S(1)} %get-tuple-element.168.middle_ref, ...), custom_call_target="tpu_custom_call" | custom-call | flops 550000000 | tf_op jit(solution)/shard_map/middle_back/pallas_call | solution.py:779
  142.9 19.3 %attend_back.3 = (bf16[768,768]{1,0:T(8,128)(2,1)}, f32[8,576]{1,0:T(8,128)}, bf16[768,768]{1,0:T(8,128)(2,1)}, f32[8,576]{1,0:T(8,128)}, f32[6,200,200]{2,1,0:T(8,128)}, /*index=5*/f32[5,200,768]{2,1,0:T(8,128)}) custom-call(s32[5]{0:T(128)S(1)} %dynamic_slice.6.refs_0_.ids_ref, ...), custom_call_target="tpu_custom_call" | custom-call | flops 2860000000 | tf_op jit(solution)/shard_map/attend_back/pallas_call | solution.py:580
  167.7 13.5 %attend_back.4 = (bf16[768,768]{1,0:T(8,128)(2,1)}, f32[8,576]{1,0:T(8,128)}, f32[3,200,200]{2,1,0:T(8,128)}, f32[5,200,768]{2,1,0:T(8,128)}) custom-call(s32[5]{0:T(128)S(1)} %dynamic_slice.6.refs_0_.ids_ref, f32[5,200,768]{2,1,0:T(8,128)} %get-tuple-element.187.refs_1_, bf16[5,200,768]{2,1,0:T(8,128)(2,1)} %get-tuple-element.143.refs_0_.refs_1_.refs_9_.refs_2_.refs_7_, ...), custom_call_target="tpu_custom_call" | custom-call | flops 1430000000 | tf_op jit(solution)/shard_map/attend_back/pallas_call | solution.py:580
  183.4 15.6 %attend_back.5 = (bf16[768,768]{1,0:T(8,128)(2,1)}, f32[8,576]{1,0:T(8,128)}, f32[3,200,200]{2,1,0:T(8,128)}, f32[5,200,768]{2,1,0:T(8,128)}, f32[16,768]{1,0:T(8,128)S(1)}, /*index=5*/f32[5,8,768]{2,1,0:T(8,128)S(1)}) custom-call(s32[5]{0:T(128)S(1)} %dynamic_slice.6.refs_0_.ids_ref, bf16[5,200,768]{2,1,0:T(8,128)(2,1)} %bitcast.31, ...), custom_call_target="tpu_custom_call" | custom-call | flops 1430000000 | tf_op jit(solution)/shard_map/attend_back/pallas_call | solution.py:580
  199.0 7.5 %table_sums.2.table0_ref = f32[72,128]{1,0:T(8,128)S(1)} custom-call(f32[3,200,200]{2,1,0:T(8,128)} %get-tuple-element.207.refs_0_, f32[6,200,200]{2,1,0:T(8,128)} %get-tuple-element.208.refs_1_.refs_3_, f32[3,200,200]{2,1,0:T(8,128)} %get-tuple-element.209.refs_2_, f32[6,200,200]{2,1,0:T(8,128)} %get-tuple-element.208.refs_1_.refs_3_, s32[200,200]{1,0:T(8,128)} %bitcast.37), custom_call_target="tpu_custom_call" | custom-call | flops 550000000 | tf_op jit(solution)/shard_map/table_sums/pallas_call | solution.py:233
  207.1 4.3 %collective-permute-done.20.c_ref = bf16[768,768]{1,0:T(8,128)(2,1)} collective-permute-done((bf16[768,768]{1,0:T(8,128)(2,1)S(1)}, bf16[768,768]{1,0:T(8,128)(2,1)}, u32[]{:S(2)}, u32[]{:S(2)}) %collective-permute-start.20) | collective-permute-done | bytes 1179680 | tf_op jit(solution)/shard_map/ppermute | solution.py:798
  217.2 5.5 %collective-permute-done.21.refs_1_ = bf16[192,768]{1,0:T(8,128)(2,1)S(1)} collective-permute-done((bf16[192,768]{1,0:T(8,128)(2,1)S(1)}, bf16[192,768]{1,0:T(8,128)(2,1)S(1)}, u32[]{:S(2)}, u32[]{:S(2)}) %collective-permute-start.21) | collective-permute-done | bytes 294944 | tf_op jit(solution)/shard_map/ppermute | solution.py:798
  228.9 8.2 %table_sums.3.table1_ref = f32[72,128]{1,0:T(8,128)S(1)} custom-call(f32[3,200,200]{2,1,0:T(8,128)} %get-tuple-element.207.refs_0_, f32[6,200,200]{2,1,0:T(8,128)} %get-tuple-element.208.refs_1_.refs_3_, f32[3,200,200]{2,1,0:T(8,128)} %get-tuple-element.209.refs_2_, f32[6,200,200]{2,1,0:T(8,128)} %get-tuple-element.208.refs_1_.refs_3_, s32[200,200]{1,0:T(8,128)} %bitcast.38), custom_call_target="tpu_custom_call" | custom-call | flops 550000000 | tf_op jit(solution)/shard_map/table_sums/pallas_call | solution.py:233
  248.2 6.6 %collective-permute-done.26.refs_1_ = bf16[96,768]{1,0:T(8,128)(2,1)S(1)} collective-permute-done((bf16[96,768]{1,0:T(8,128)(2,1)S(1)}, bf16[96,768]{1,0:T(8,128)(2,1)S(1)}, u32[]{:S(2)}, u32[]{:S(2)}) %collective-permute-start.26) | collective-permute-done | bytes 147488 | tf_op jit(solution)/shard_map/ppermute | solution.py:798
  257.2 3.2 %collective-permute-done.31 = f32[24,768]{1,0:T(8,128)S(1)} collective-permute-done((f32[24,768]{1,0:T(8,128)S(1)}, f32[24,768]{1,0:T(8,128)S(1)}, u32[]{:S(2)}, u32[]{:S(2)}) %collective-permute-start.31) | collective-permute-done | bytes 73760 | tf_op jit(solution)/shard_map/ppermute | solution.py:798
  260.4 4.5 %collective-permute-done.29.refs_1_ = bf16[96,768]{1,0:T(8,128)(2,1)S(1)} collective-permute-done((bf16[96,768]{1,0:T(8,128)(2,1)S(1)}, bf16[96,768]{1,0:T(8,128)(2,1)S(1)}, u32[]{:S(2)}, u32[]{:S(2)}) %collective-permute-start.29) | collective-permute-done | bytes 147488 | tf_op jit(solution)/shard_map/ppermute | solution.py:798
  270.1 21.2 %collective-permute-done.34 = f32[24,768]{1,0:T(8,128)S(1)} collective-permute-done((f32[24,768]{1,0:T(8,128)S(1)}, f32[24,768]{1,0:T(8,128)S(1)}, u32[]{:S(2)}, u32[]{:S(2)}) %collective-permute-start.34) | collective-permute-done | bytes 73760 | tf_op jit(solution)/shard_map/ppermute | solution.py:798
  293.5 7.7 %collective-permute-done.35.got_ref = f32[24,768]{1,0:T(8,128)S(1)} collective-permute-done((f32[24,768]{1,0:T(8,128)S(1)}, f32[24,768]{1,0:T(8,128)S(1)}, u32[]{:S(2)}, u32[]{:S(2)}) %collective-permute-start.35) | collective-permute-done | bytes 73760 | tf_op jit(solution)/shard_map/ppermute | solution.py:798
  (156 shorter events, 79.2 us)
Async XLA Ops:
  7.2 298.6 %all-reduce.3.cloned.1.call-start = ((), (), s32[]{:S(2)}) async-start(), calls=%async_computation | async-start | bytes 4718592 | tf_op jit(solution)/shard_map/psum | solution.py:1130
  9.2 25.3 %collective-permute-start.2 = (bf16[768,768]{1,0:T(8,128)(2,1)S(1)}, bf16[768,768]{1,0:T(8,128)(2,1)}, u32[]{:S(2)}, u32[]{:S(2)}) collective-permute-start(bf16[768,768]{1,0:T(8,128)(2,1)S(1)} %get-tuple-element.147), channel_id=1, source_target_pairs={{0,1},{1,0},{2,3},{3,2},{4,5},{5,4},{6,7},{7,6},{8,9},{9,8},{10,11... | collective-permute-start | bytes 3538952 | tf_op jit(solution)/shard_map/ppermute | solution.py:798
  9.7 21.2 %collective-permute-start.1 = (bf16[400,768]{1,0:T(8,128)(2,1)S(1)}, bf16[400,768]{1,0:T(8,128)(2,1)}, u32[]{:S(2)}, u32[]{:S(2)}) collective-permute-start(bf16[400,768]{1,0:T(8,128)(2,1)S(1)} %get-tuple-element.145), channel_id=1, source_target_pairs={{0,2},{1,3},{2,0},{3,1},{4,6},{5,7},{6,4},{7,5},{8,10},{9,11},{10,... | collective-permute-start | bytes 1843208 | tf_op jit(solution)/shard_map/ppermute | solution.py:798
  30.9 16.4 %collective-permute-start.3 = (bf16[400,768]{1,0:T(8,128)(2,1)}, bf16[400,768]{1,0:T(8,128)(2,1)S(1)}, u32[]{:S(2)}, u32[]{:S(2)}) collective-permute-start(bf16[400,768]{1,0:T(8,128)(2,1)} %collective-permute-done.1.near_ref.refs_3_.refs_5_.refs_11_), channel_id=1, source_target_pairs={{0,4},{4,0},{8,12},{12,8},{16,20},{20,16},{24,28},{28,24},{1,5},{5... | collective-permute-start | bytes 1843208 | tf_op jit(solution)/shard_map/ppermute | solution.py:798
  32.4 14.8 %collective-permute-start.4 = (bf16[400,768]{1,0:T(8,128)(2,1)}, bf16[400,768]{1,0:T(8,128)(2,1)S(1)}, u32[]{:S(2)}, u32[]{:S(2)}) collective-permute-start(bf16[400,768]{1,0:T(8,128)(2,1)} %collective-permute-done.1.near_ref.refs_3_.refs_5_.refs_11_), channel_id=1, source_target_pairs={{0,1},{1,0},{2,3},{3,2},{4,5},{5,4},{6,7},{7,6},{8,9},{9,8},{10,11... | collective-permute-start | bytes 1843208 | tf_op jit(solution)/shard_map/ppermute | solution.py:798
  32.5 28.2 %collective-permute-start.5 = (bf16[768,384]{1,0:T(8,128)(2,1)S(1)}, bf16[768,384]{1,0:T(8,128)(2,1)S(1)}, u32[]{:S(2)}, u32[]{:S(2)}) collective-permute-start(bf16[768,384]{1,0:T(8,128)(2,1)S(1)} %get-tuple-element.153), channel_id=1, source_target_pairs={{0,2},{1,3},{2,0},{3,1},{4,6},{5,7},{6,4},{7,5},{8,10},{9,11},{10,... | collective-permute-start | bytes 1769480 | tf_op jit(solution)/shard_map/ppermute | solution.py:798
  33.0 41.6 %collective-permute-start.7 = (bf16[768,768]{1,0:T(8,128)(2,1)S(1)}, bf16[768,768]{1,0:T(8,128)(2,1)S(1)}, u32[]{:S(2)}, u32[]{:S(2)}) collective-permute-start(bf16[768,768]{1,0:T(8,128)(2,1)S(1)} %copy-done.12), channel_id=1, source_target_pairs={{0,2},{1,3},{2,0},{3,1},{4,6},{5,7},{6,4},{7,5},{8,10},{9,11},{10,... | collective-permute-start | bytes 3538952 | tf_op jit(solution)/shard_map/ppermute | solution.py:798
  47.2 15.0 %collective-permute-start.6 = (bf16[400,768]{1,0:T(8,128)(2,1)S(1)}, bf16[400,768]{1,0:T(8,128)(2,1)S(1)}, u32[]{:S(2)}, u32[]{:S(2)}) collective-permute-start(bf16[400,768]{1,0:T(8,128)(2,1)S(1)} %collective-permute-done.3.refs_4_), channel_id=1, source_target_pairs={{0,1},{1,0},{2,3},{3,2},{4,5},{5,4},{6,7},{7,6},{8,9},{9,8},{10,11... | collective-permute-start | bytes 1843208 | tf_op jit(solution)/shard_map/ppermute | solution.py:798
  60.7 15.8 %collective-permute-start.8 = (bf16[768,384]{1,0:T(8,128)(2,1)S(1)}, bf16[768,384]{1,0:T(8,128)(2,1)S(1)}, u32[]{:S(2)}, u32[]{:S(2)}) collective-permute-start(bf16[768,384]{1,0:T(8,128)(2,1)S(1)} %collective-permute-done.5.refs_9_), channel_id=1, source_target_pairs={{0,4},{4,0},{8,12},{12,8},{16,20},{20,16},{24,28},{28,24},{1,5},{5... | collective-permute-start | bytes 1769480 | tf_op jit(solution)/shard_map/ppermute | solution.py:798
  103.1 9.2 %collective-permute-start.13 = (bf16[768,768]{1,0:T(8,128)(2,1)S(1)}, bf16[768,768]{1,0:T(8,128)(2,1)S(1)}, u32[]{:S(2)}, u32[]{:S(2)}) collective-permute-start(bf16[768,768]{1,0:T(8,128)(2,1)S(1)} %copy-done.12), channel_id=1, source_target_pairs={{0,1},{1,0},{2,3},{3,2},{4,5},{5,4},{6,7},{7,6},{8,9},{9,8},{10,11... | collective-permute-start | bytes 3538952 | tf_op jit(solution)/shard_map/ppermute | solution.py:798
  112.0 53.4 %collective-permute-start.17 = (bf16[1536,768]{1,0:T(8,128)(2,1)S(1)}, bf16[1536,768]{1,0:T(8,128)(2,1)S(1)}, u32[]{:S(2)}, u32[]{:S(2)}) collective-permute-start(bf16[1536,768]{1,0:T(8,128)(2,1)S(1)} %add_convert_fusion), channel_id=1, source_target_pairs={{0,2},{1,3},{2,0},{3,1},{4,6},{5,7},{6,4},{7,5},{8,10},{9,11},{10,... | collective-permute-start | bytes 7077896 | tf_op jit(solution)/shard_map/ppermute | solution.py:798
  162.2 19.0 %collective-permute-start.18 = (bf16[768,768]{1,0:T(8,128)(2,1)}, bf16[768,768]{1,0:T(8,128)(2,1)S(1)}, u32[]{:S(2)}, u32[]{:S(2)}) collective-permute-start(bf16[768,768]{1,0:T(8,128)(2,1)} %get-tuple-element.194), channel_id=1, source_target_pairs={{0,1},{1,0},{2,3},{3,2},{4,5},{5,4},{6,7},{7,6},{8,9},{9,8},{10,11... | collective-permute-start | bytes 3538952 | tf_op jit(solution)/shard_map/ppermute | solution.py:798
  182.8 24.3 %collective-permute-start.19 = (bf16[768,768]{1,0:T(8,128)(2,1)}, bf16[768,768]{1,0:T(8,128)(2,1)S(1)}, u32[]{:S(2)}, u32[]{:S(2)}) collective-permute-start(bf16[768,768]{1,0:T(8,128)(2,1)} %get-tuple-element.205), channel_id=1, source_target_pairs={{0,1},{1,0},{2,3},{3,2},{4,5},{5,4},{6,7},{7,6},{8,9},{9,8},{10,11... | collective-permute-start | bytes 3538952 | tf_op jit(solution)/shard_map/ppermute | solution.py:798
  182.9 28.5 %collective-permute-start.20 = (bf16[768,768]{1,0:T(8,128)(2,1)S(1)}, bf16[768,768]{1,0:T(8,128)(2,1)}, u32[]{:S(2)}, u32[]{:S(2)}) collective-permute-start(bf16[768,768]{1,0:T(8,128)(2,1)S(1)} %add_convert_fusion.1), channel_id=1, source_target_pairs={{0,2},{1,3},{2,0},{3,1},{4,6},{5,7},{6,4},{7,5},{8,10},{9,11},{10,... | collective-permute-start | bytes 3538952 | tf_op jit(solution)/shard_map/ppermute | solution.py:798
  224.9 16.3 %collective-permute-start.23 = (bf16[96,768]{1,0:T(8,128)(2,1)S(1)}, bf16[96,768]{1,0:T(8,128)(2,1)S(1)}, u32[]{:S(2)}, u32[]{:S(2)}) collective-permute-start(bf16[96,768]{1,0:T(8,128)(2,1)S(1)} %get-tuple-element.225), channel_id=1, source_target_pairs={{0,8},{4,12},{8,0},{12,4},{16,24},{20,28},{24,16},{28,20},{1,9},{5... | collective-permute-start | bytes 442376 | tf_op jit(solution)/shard_map/ppermute | solution.py:798
  226.4 14.9 %collective-permute-start.24 = (bf16[96,768]{1,0:T(8,128)(2,1)S(1)}, bf16[96,768]{1,0:T(8,128)(2,1)S(1)}, u32[]{:S(2)}, u32[]{:S(2)}) collective-permute-start(bf16[96,768]{1,0:T(8,128)(2,1)S(1)} %get-tuple-element.226), channel_id=1, source_target_pairs={{0,16},{4,20},{8,24},{12,28},{16,0},{20,4},{24,8},{28,12},{1,17},{... | collective-permute-start | bytes 442376 | tf_op jit(solution)/shard_map/ppermute | solution.py:798
  242.8 12.0 %collective-permute-start.26 = (bf16[96,768]{1,0:T(8,128)(2,1)S(1)}, bf16[96,768]{1,0:T(8,128)(2,1)S(1)}, u32[]{:S(2)}, u32[]{:S(2)}) collective-permute-start(bf16[96,768]{1,0:T(8,128)(2,1)S(1)} %get-tuple-element.233.refs_0_), channel_id=1, source_target_pairs={{0,16},{4,20},{8,24},{12,28},{16,0},{20,4},{24,8},{28,12},{1,17},{... | collective-permute-start | bytes 442376 | tf_op jit(solution)/shard_map/ppermute | solution.py:798
  243.2 11.6 %collective-permute-start.27 = (bf16[96,768]{1,0:T(8,128)(2,1)S(1)}, bf16[96,768]{1,0:T(8,128)(2,1)S(1)}, u32[]{:S(2)}, u32[]{:S(2)}) collective-permute-start(bf16[96,768]{1,0:T(8,128)(2,1)S(1)} %get-tuple-element.234.refs_2_), channel_id=1, source_target_pairs={{0,4},{4,0},{8,12},{12,8},{16,20},{20,16},{24,28},{28,24},{1,5},{5... | collective-permute-start | bytes 442376 | tf_op jit(solution)/shard_map/ppermute | solution.py:798
  255.4 9.4 %collective-permute-start.29 = (bf16[96,768]{1,0:T(8,128)(2,1)S(1)}, bf16[96,768]{1,0:T(8,128)(2,1)S(1)}, u32[]{:S(2)}, u32[]{:S(2)}) collective-permute-start(bf16[96,768]{1,0:T(8,128)(2,1)S(1)} %get-tuple-element.238.refs_0_), channel_id=1, source_target_pairs={{0,8},{4,12},{8,0},{12,4},{16,24},{20,28},{24,16},{28,20},{1,9},{5... | collective-permute-start | bytes 442376 | tf_op jit(solution)/shard_map/ppermute | solution.py:798
  255.5 11.8 %collective-permute-start.30 = (bf16[96,768]{1,0:T(8,128)(2,1)S(1)}, bf16[96,768]{1,0:T(8,128)(2,1)S(1)}, u32[]{:S(2)}, u32[]{:S(2)}) collective-permute-start(bf16[96,768]{1,0:T(8,128)(2,1)S(1)} %get-tuple-element.239.refs_2_), channel_id=1, source_target_pairs={{0,16},{4,20},{8,24},{12,28},{16,0},{20,4},{24,8},{28,12},{1,17},{... | collective-permute-start | bytes 442376 | tf_op jit(solution)/shard_map/ppermute | solution.py:798
  267.9 23.4 %collective-permute-start.32 = (bf16[192,768]{1,0:T(8,128)(2,1)S(1)}, bf16[192,768]{1,0:T(8,128)(2,1)S(1)}, u32[]{:S(2)}, u32[]{:S(2)}) collective-permute-start(bf16[192,768]{1,0:T(8,128)(2,1)S(1)} %get-tuple-element.243.refs_0_), channel_id=1, source_target_pairs={{0,4},{4,0},{8,12},{12,8},{16,20},{20,16},{24,28},{28,24},{1,5},{5... | collective-permute-start | bytes 884744 | tf_op jit(solution)/shard_map/ppermute | solution.py:798
  268.0 23.3 %collective-permute-start.33 = (bf16[192,768]{1,0:T(8,128)(2,1)S(1)}, bf16[192,768]{1,0:T(8,128)(2,1)S(1)}, u32[]{:S(2)}, u32[]{:S(2)}) collective-permute-start(bf16[192,768]{1,0:T(8,128)(2,1)S(1)} %get-tuple-element.244.refs_2_), channel_id=1, source_target_pairs={{0,8},{4,12},{8,0},{12,4},{16,24},{20,28},{24,16},{28,20},{1,9},{5... | collective-permute-start | bytes 884744 | tf_op jit(solution)/shard_map/ppermute | solution.py:798
  268.4 22.9 %collective-permute-start.34 = (f32[24,768]{1,0:T(8,128)S(1)}, f32[24,768]{1,0:T(8,128)S(1)}, u32[]{:S(2)}, u32[]{:S(2)}) collective-permute-start(f32[24,768]{1,0:T(8,128)S(1)} %add.47), channel_id=1, source_target_pairs={{0,8},{4,12},{8,0},{12,4},{16,24},{20,28},{24,16},{28,20},{1,9},{5... | collective-permute-start | bytes 221192 | tf_op jit(solution)/shard_map/ppermute | solution.py:798
  291.3 9.9 %collective-permute-start.35 = (f32[24,768]{1,0:T(8,128)S(1)}, f32[24,768]{1,0:T(8,128)S(1)}, u32[]{:S(2)}, u32[]{:S(2)}) collective-permute-start(f32[24,768]{1,0:T(8,128)S(1)} %add.48.held_ref), channel_id=1, source_target_pairs={{0,16},{4,20},{8,24},{12,28},{16,0},{20,4},{24,8},{28,12},{1,17},{... | collective-permute-start | bytes 221192 | tf_op jit(solution)/shard_map/ppermute | solution.py:798
  (44 other events, 433.4 us)
Sparse Core Ops, SparseCore 0:
  183.4 122.3 all-reduce.2
where the time goes:
time: 319 us; the launch traced here: 317 us
  Pallas kernels  170 us (53%)
  waiting for transfers between devices  82.8 us (26%)
  starting transfers between devices  25 us (8%)
  between operations  14.6 us (5%)
  other arithmetic  12.6 us (4%)
  local copies, waits for them, and re-layouts  12.4 us (4%)
    ppermute x36, waiting for transfers between devices, swap(): return lax.ppermute(values, axis, [(i, i ^ mask) for i in range(count)])  80.4 us
    pallas_call x3, Pallas kernels, attend_back(): pl.pallas_call(functools.partial(attend_back_kernel, first, last, count),...  48.4 us
    pallas_call x2, Pallas kernels, mlp(): pl.pallas_call(functools.partial(mlp_kernel, first, [len(shard) for shard...  40.1 us
    pallas_call x4, Pallas kernels, attend(): pl.pallas_call(functools.partial(attend_kernel, first, last, parted), out...  39.6 us
    ppermute x36, starting transfers between devices, swap(): return lax.ppermute(values, axis, [(i, i ^ mask) for i in range(count)])  24.9 us
    pallas_call x2, Pallas kernels, table_sums(): pl.pallas_call(table_kernel, out_shape=shaped((chunks * heads, LANES), F3...  15.7 us
    unnamed x63, local copies, waits for them, and re-layouts  8.27 us
    pallas_call x6, Pallas kernels, step_call(): pl.pallas_call(kernel, out_shape=outs, in_specs=[pl.BlockSpec(memory_spac...  7.36 us
  transfers between devices with their start and end apart: 37, of which 18 were waited for; matrix products, arithmetic and copies ran while one was open for 4% of the time, Pallas kernels for 47%

commit v1 on v0

--- a/solution.py
+++ b/solution.py
@@ -1080,15 +1080,15 @@
     attn_p3 = swap(attn_p2, "mp", 1)
     small2, small3 = (attn_p2, 2 * own // SMALL_ROWS), (attn_p3, 2 * own // SMALL_ROWS)
     j1, probs1, c1, part = attend(mix, norm1, pack1, (pack1, 3), small1, bias_near, 1, mask, x1, part)
-    part, attn_q2 = lax.optimization_barrier((part, attn_q2))
+    part, index = lax.optimization_barrier((part, index))
+    bias_far = position_bias([small2, small3], 2 * own_heads, index)
+    part, bias_far, attn_q2, down_p2 = lax.optimization_barrier((part, bias_far, attn_q2, down_p2))
     attn_q3 = swap(attn_q2, "mp", 1)
-    bias_far = position_bias([small2, small3], 2 * own_heads, index)
+    down_q2 = swap(down_p2, "dp", 1)
+    down_p3 = swap(down_p2, "mp", 1)
     j2, probs2, c2, part, pack2 = attend(
         mix, norm1, attn_p2, attn_q2, small2, bias_far, 0, mask, x1, part, side
     )
-    part, down_p2 = lax.optimization_barrier((part, down_p2))
-    down_q2 = swap(down_p2, "dp", 1)
-    down_p3 = swap(down_p2, "mp", 1)
     j3, probs3, c3, attn_value, middle, normed2, pack3 = attend(
         mix, [norm2_gain, norm2_shift], attn_p3, attn_q3, small3, bias_far, 1, mask, x1, part, side,
         [out_bias, gamma_attn],
@@ -1151,8 +1151,14 @@
     )
     tail.go_on()
     small = Chain(small_chain(held, sent, 16, 8))
+    joint = 0
     while tail.done is None or small.done is None:
         going = [chain for chain in (tail, small) if chain.done is None]
+        joint += 1
+        if joint == 3:
+            going[0].got[0], up_sum, down_sum = lax.optimization_barrier(
+                (going[0].got[0], up_sum, down_sum)
+            )
         together(*going)
         for chain in going:
             chain.go_on()

time: 319 us -> 313 us (0.981)
  waiting for transfers between devices: 82.8 us -> 73.4 us
    ppermute x36, waiting for transfers between devices: 80.4 us -> 59.5 us  [swap(): return lax.ppermute(values, axis, [(i, i ^ mask) for i in range(count)])]
    psum x1, waiting for transfers between devices: 2.41 us -> 13.9 us  [local(): up_sum, down_sum = lax.psum(tuple(mlp_sum), 'dp')]
  transfers between devices with their start and end apart: 37 -> 37, of which waited for: 18 -> 16; matrix products, arithmetic and copies ran while one was open for 4% -> 6% of each run, Pallas kernels for 47% -> 47%
where the time goes in v1:
time: 313 us; the launch traced here: 311 us
  Pallas kernels  170 us (54%)
  waiting for transfers between devices  73.4 us (23%)
  starting transfers between devices  27.8 us (9%)
  between operations  14.5 us (5%)
  local copies, waits for them, and re-layouts  12.5 us (4%)
  other arithmetic  12.5 us (4%)
    ppermute x36, waiting for transfers between devices, swap(): return lax.ppermute(values, axis, [(i, i ^ mask) for i in range(count)])  59.5 us
    pallas_call x3, Pallas kernels, attend_back(): pl.pallas_call(functools.partial(attend_back_kernel, first, last, count),...  48.2 us
    pallas_call x2, Pallas kernels, mlp(): pl.pallas_call(functools.partial(mlp_kernel, first, [len(shard) for shard...  40.1 us
    pallas_call x4, Pallas kernels, attend(): pl.pallas_call(functools.partial(attend_kernel, first, last, parted), out...  39.7 us
    ppermute x36, starting transfers between devices, swap(): return lax.ppermute(values, axis, [(i, i ^ mask) for i in range(count)])  27.8 us
    pallas_call x2, Pallas kernels, table_sums(): pl.pallas_call(table_kernel, out_shape=shaped((chunks * heads, LANES), F3...  15.6 us
    psum x1, waiting for transfers between devices, local(): up_sum, down_sum = lax.psum(tuple(mlp_sum), 'dp')  13.9 us
    unnamed x63, local copies, waits for them, and re-layouts  8.37 us
  transfers between devices with their start and end apart: 37, of which 16 were waited for; matrix products, arithmetic and copies ran while one was open for 6% of the time, Pallas kernels for 47%

profile of v1, /device:TPU:0, one launch (start us, length us, event | category | flops | bytes accessed | tf_op | source)
XLA Modules:
  0.0 310.7 jit_solution(6745443255387102530)
XLA Ops:
  16.9 3.4 %position_bias.2.refs_9_.refs_5_ = f32[6,200,256]{2,1,0:T(8,128)S(1)} custom-call(bf16[16,768]{1,0:T(8,128)(2,1)} %copy-done, bf16[16,768]{1,0:T(8,128)(2,1)} %copy-done.25, s32[200,200]{1,0:T(8,128)} %bitcast.35), custom_call_target="tpu_custom_call" | custom-call | flops 220000000 | tf_op jit(solution)/shard_map/position_bias/pallas_call | solution.py:194
  20.3 10.5 %attend.4 = (bf16[5,200,768]{2,1,0:T(8,128)(2,1)}, bf16[5,200,576]{2,1,0:T(8,128)(2,1)}, bf16[5,3,200,200]{3,2,1,0:T(8,128)(2,1)}, bf16[5,200,192]{2,1,0:T(8,128)(2,1)}, f32[5,200,768]{2,1,0:T(8,128)S(1)}) custom-call(s32[5]{0:T(128)S(1)} %dynamic_slice.6.refs_0_.ids_ref, bf16[5,200,768]{2,1,0:T(8,128)(2,1)} %bitcast.29, f32[8,200,1]{2,1,0:T(8,128)} %copy.50.refs_2_.refs_3_, ...), custom_call_target="tpu_custom_call" | custom-call | flops 990000000 | tf_op jit(solution)/shard_map/attend/pallas_call | solution.py:408
  34.8 8.5 %attend.5 = (bf16[5,200,576]{2,1,0:T(8,128)(2,1)}, bf16[5,3,200,200]{3,2,1,0:T(8,128)(2,1)}, bf16[5,200,192]{2,1,0:T(8,128)(2,1)}, f32[5,200,768]{2,1,0:T(8,128)S(1)}) custom-call(bf16[5,200,768]{2,1,0:T(8,128)(2,1)} %get-tuple-element.148.refs_0_.refs_1_.refs_9_.refs_2_.refs_7_, f32[5,200,768]{2,1,0:T(8,128)S(1)} %get-tuple-element.151.refs_1_, ...), custom_call_target="tpu_custom_call" | custom-call | flops 990000000 | tf_op jit(solution)/shard_map/attend/pallas_call | solution.py:408
  44.2 3.4 %position_bias.3.refs_6_.refs_14_ = f32[6,200,256]{2,1,0:T(8,128)S(1)} custom-call(bf16[400,768]{1,0:T(8,128)(2,1)} %collective-permute-done.1.near_ref.refs_3_.refs_5_.refs_11_, bf16[400,768]{1,0:T(8,128)(2,1)} %copy-done.9, s32[200,200]{1,0:T(8,128)} %bitcast.36), custom_call_target="tpu_custom_call" | custom-call | flops 220000000 | tf_op jit(solution)/shard_map/position_bias/pallas_call | solution.py:194
  49.9 9.1 %attend.6 = (bf16[5,200,576]{2,1,0:T(8,128)(2,1)}, bf16[5,3,200,200]{3,2,1,0:T(8,128)(2,1)}, bf16[5,200,192]{2,1,0:T(8,128)(2,1)}, f32[5,200,768]{2,1,0:T(8,128)S(1)}, bf16[768,768]{1,0:T(8,128)(2,1)}) custom-call(s32[1]{0:T(128)} %bitcast.side_ref.refs_0_.refs_1_, bf16[5,200,768]{2,1,0:T(8,128)(2,1)} %get-tuple-element.148.refs_0_.refs_1_.refs_9_.refs_2_.refs_7_, ...), custom_call_target="tpu_custom_call" | custom-call | flops 990000000 | tf_op jit(solution)/shard_map/attend/pallas_call | solution.py:408
  59.8 11.5 %attend.7 = (bf16[5,200,576]{2,1,0:T(8,128)(2,1)}, bf16[5,3,200,200]{3,2,1,0:T(8,128)(2,1)}, bf16[5,200,192]{2,1,0:T(8,128)(2,1)}, f32[5,200,768]{2,1,0:T(8,128)...) custom-call(s32[5]{0:T(128)S(1)} %dynamic_slice.6.refs_0_.ids_ref, ...), custom_call_target="tpu_custom_call" | custom-call | flops 990000000 | tf_op jit(solution)/shard_map/attend/pallas_call | solution.py:408
  73.9 3.1 collective-permute-done.10.refs_5_
  79.6 20.0 %mlp.2 = (f32[1000,768]{1,0:T(8,128)S(1)}, f32[1000,768]{1,0:T(8,128)S(1)}, bf16[1536,768]{1,0:T(8,128)(2,1)}, bf16[1536,768]{1,0:T(8,128)(2,1)}, f32[16,768]{1,0:T(8,128)S(1)}) custom-call(s32[1]{0:T(128)} %bitcast.side_ref.refs_0_.refs_1_, bf16[1000,768]{1,0:T(8,128)(2,1)S(1)} %bitcast.26, bf16[1000,768]{1,0:T(8,128)(2,1)} %refs_2_.3, f32[768]{0:T(1024)} %gmlp_ref.1, ...), custom_call_target="tpu_custom_call" | custom-call | flops 1980000000 | tf_op jit(solution)/shard_map/mlp/pallas_call | solution.py:717
  100.4 6.1 %collective-permute-done.12 = bf16[1536,768]{1,0:T(8,128)(2,1)S(1)} collective-permute-done((bf16[1536,768]{1,0:T(8,128)(2,1)}, bf16[1536,768]{1,0:T(8,128)(2,1)S(1)}, u32[]{:S(2)}, u32[]{:S(2)}) %collective-permute-start.12) | collective-permute-done | bytes 2359328 | tf_op jit(solution)/shard_map/ppermute | solution.py:798
  110.8 20.1 %mlp.3 = (f32[1000,768]{1,0:T(8,128)S(1)}, f32[1000,768]{1,0:T(8,128)S(1)}, bf16[1536,768]{1,0:T(8,128)(2,1)}, bf16[1536,768]{1,0:T(8,128)(2,1)}, f32[16,768]{1,0:T(8,128)S(1)}) custom-call(s32[1]{0:T(128)} %bitcast.side_ref.refs_0_.refs_1_, bf16[1000,768]{1,0:T(8,128)(2,1)S(1)} %bitcast.27, ...), custom_call_target="tpu_custom_call", output_to_operand_aliasing={{0}: (10, {}), {1}: (11, {})} | custom-call | flops 1980000000 | tf_op jit(solution)/shard_map/mlp/pallas_call | solution.py:717
  133.2 6.7 %middle_back.1 = (bf16[5,200,768]{2,1,0:T(8,128)(2,1)}, f32[5,200,768]{2,1,0:T(8,128)}, bf16[5,200,768]{2,1,0:T(8,128)(2,1)}, f32[48,768]{1,0:T(8,128)S(1)}) custom-call(f32[5,200,768]{2,1,0:T(8,128)S(1)} %bitcast.24, f32[5,200,768]{2,1,0:T(8,128)S(1)} %bitcast.25, f32[5,200,768]{2,1,0:T(8,128)S(1)} %get-tuple-element.175.middle_ref, ...), custom_call_target="tpu_custom_call" | custom-call | flops 550000000 | tf_op jit(solution)/shard_map/middle_back/pallas_call | solution.py:779
  140.0 19.3 %attend_back.3 = (bf16[768,768]{1,0:T(8,128)(2,1)}, f32[8,576]{1,0:T(8,128)}, bf16[768,768]{1,0:T(8,128)(2,1)}, f32[8,576]{1,0:T(8,128)}, f32[6,200,200]{2,1,0:T(8,128)}, /*index=5*/f32[5,200,768]{2,1,0:T(8,128)}) custom-call(s32[5]{0:T(128)S(1)} %dynamic_slice.6.refs_0_.ids_ref, ...), custom_call_target="tpu_custom_call" | custom-call | flops 2860000000 | tf_op jit(solution)/shard_map/attend_back/pallas_call | solution.py:580
  164.5 13.5 %attend_back.4 = (bf16[768,768]{1,0:T(8,128)(2,1)}, f32[8,576]{1,0:T(8,128)}, f32[3,200,200]{2,1,0:T(8,128)}, f32[5,200,768]{2,1,0:T(8,128)}) custom-call(s32[5]{0:T(128)S(1)} %dynamic_slice.6.refs_0_.ids_ref, f32[5,200,768]{2,1,0:T(8,128)} %get-tuple-element.194.refs_1_, bf16[5,200,768]{2,1,0:T(8,128)(2,1)} %get-tuple-element.148.refs_0_.refs_1_.refs_9_.refs_2_.refs_7_, ...), custom_call_target="tpu_custom_call" | custom-call | flops 1430000000 | tf_op jit(solution)/shard_map/attend_back/pallas_call | solution.py:580
  180.6 15.4 %attend_back.5 = (bf16[768,768]{1,0:T(8,128)(2,1)}, f32[8,576]{1,0:T(8,128)}, f32[3,200,200]{2,1,0:T(8,128)}, f32[5,200,768]{2,1,0:T(8,128)}, f32[16,768]{1,0:T(8,128)S(1)}, /*index=5*/f32[5,8,768]{2,1,0:T(8,128)S(1)}) custom-call(s32[5]{0:T(128)S(1)} %dynamic_slice.6.refs_0_.ids_ref, bf16[5,200,768]{2,1,0:T(8,128)(2,1)} %bitcast.31, ...), custom_call_target="tpu_custom_call" | custom-call | flops 1430000000 | tf_op jit(solution)/shard_map/attend_back/pallas_call | solution.py:580
  196.0 7.5 %table_sums.2.table0_ref = f32[72,128]{1,0:T(8,128)S(1)} custom-call(f32[3,200,200]{2,1,0:T(8,128)} %get-tuple-element.214.refs_0_, f32[6,200,200]{2,1,0:T(8,128)} %get-tuple-element.215.refs_1_.refs_3_, f32[3,200,200]{2,1,0:T(8,128)} %get-tuple-element.216.refs_2_, f32[6,200,200]{2,1,0:T(8,128)} %get-tuple-element.215.refs_1_.refs_3_, s32[200,200]{1,0:T(8,128)} %bitcast.37), custom_call_target="tpu_custom_call" | custom-call | flops 550000000 | tf_op jit(solution)/shard_map/table_sums/pallas_call | solution.py:233
  204.1 4.2 %collective-permute-done.20.c_ref = bf16[768,768]{1,0:T(8,128)(2,1)} collective-permute-done((bf16[768,768]{1,0:T(8,128)(2,1)S(1)}, bf16[768,768]{1,0:T(8,128)(2,1)}, u32[]{:S(2)}, u32[]{:S(2)}) %collective-permute-start.20) | collective-permute-done | bytes 1179680 | tf_op jit(solution)/shard_map/ppermute | solution.py:798
  213.3 6.2 %collective-permute-done.21.refs_1_ = bf16[192,768]{1,0:T(8,128)(2,1)S(1)} collective-permute-done((bf16[192,768]{1,0:T(8,128)(2,1)S(1)}, bf16[192,768]{1,0:T(8,128)(2,1)S(1)}, u32[]{:S(2)}, u32[]{:S(2)}) %collective-permute-start.21) | collective-permute-done | bytes 294944 | tf_op jit(solution)/shard_map/ppermute | solution.py:798
  226.1 8.2 %table_sums.3.table1_ref = f32[72,128]{1,0:T(8,128)S(1)} custom-call(f32[3,200,200]{2,1,0:T(8,128)} %get-tuple-element.214.refs_0_, f32[6,200,200]{2,1,0:T(8,128)} %get-tuple-element.215.refs_1_.refs_3_, f32[3,200,200]{2,1,0:T(8,128)} %get-tuple-element.216.refs_2_, f32[6,200,200]{2,1,0:T(8,128)} %get-tuple-element.215.refs_1_.refs_3_, s32[200,200]{1,0:T(8,128)} %bitcast.38), custom_call_target="tpu_custom_call" | custom-call | flops 550000000 | tf_op jit(solution)/shard_map/table_sums/pallas_call | solution.py:233
  242.8 3.1 %collective-permute-done.28 = f32[24,768]{1,0:T(8,128)S(1)} collective-permute-done((f32[24,768]{1,0:T(8,128)S(1)}, f32[24,768]{1,0:T(8,128)S(1)}, u32[]{:S(2)}, u32[]{:S(2)}) %collective-permute-start.28) | collective-permute-done | bytes 73760 | tf_op jit(solution)/shard_map/ppermute | solution.py:798
  246.0 6.2 %collective-permute-done.26.refs_1_ = bf16[96,768]{1,0:T(8,128)(2,1)S(1)} collective-permute-done((bf16[96,768]{1,0:T(8,128)(2,1)S(1)}, bf16[96,768]{1,0:T(8,128)(2,1)S(1)}, u32[]{:S(2)}, u32[]{:S(2)}) %collective-permute-start.26) | collective-permute-done | bytes 147488 | tf_op jit(solution)/shard_map/ppermute | solution.py:798
  252.9 4.2 %collective-permute-start.30 = (bf16[96,768]{1,0:T(8,128)(2,1)S(1)}, bf16[96,768]{1,0:T(8,128)(2,1)S(1)}, u32[]{:S(2)}, u32[]{:S(2)}) collective-permute-start(bf16[96,768]{1,0:T(8,128)(2,1)S(1)} %get-tuple-element.249.refs_2_), channel_id=1, source_target_pairs={{0,16},{4,20},{8,24},{12,28},{16,0},{20,4},{24,8},{28,12},{1,17},{... | collective-permute-start | bytes 442376 | tf_op jit(solution)/shard_map/ppermute | solution.py:798
  257.2 11.3 %collective-permute-done.29.refs_1_ = bf16[96,768]{1,0:T(8,128)(2,1)S(1)} collective-permute-done((bf16[96,768]{1,0:T(8,128)(2,1)S(1)}, bf16[96,768]{1,0:T(8,128)(2,1)S(1)}, u32[]{:S(2)}, u32[]{:S(2)}) %collective-permute-start.29) | collective-permute-done | bytes 147488 | tf_op jit(solution)/shard_map/ppermute | solution.py:798
  268.5 13.9 %all-reduce.3.cloned.1.call-done = (bf16[768,768]{1,0:T(8,128)(2,1)}, bf16[768,768]{1,0:T(8,128)(2,1)}) async-done(((bf16[768,768]{1,0:T(8,128)(2,1)}, bf16[768,768]{1,0:T(8,128)(2,1)}), (bf16[768,768]{1,0:T(8,128)(2,1)}, bf16[768,768]{1,0:T(8,128)(2,1)})) %all-reduce.3.cloned.1.call-update) | async-done | bytes 2359312 | tf_op jit(solution)/shard_map/psum | solution.py:1130
  285.9 8.2 %collective-permute-done.34 = f32[24,768]{1,0:T(8,128)S(1)} collective-permute-done((f32[24,768]{1,0:T(8,128)S(1)}, f32[24,768]{1,0:T(8,128)S(1)}, u32[]{:S(2)}, u32[]{:S(2)}) %collective-permute-start.34) | collective-permute-done | bytes 73760 | tf_op jit(solution)/shard_map/ppermute | solution.py:798
  (156 shorter events, 72.7 us)
Async XLA Ops:
  7.2 275.1 %all-reduce.3.cloned.1.call-start = ((), (), s32[]{:S(2)}) async-start(), calls=%async_computation | async-start | bytes 4718592 | tf_op jit(solution)/shard_map/psum | solution.py:1130
  9.2 25.6 %collective-permute-start.2 = (bf16[768,768]{1,0:T(8,128)(2,1)S(1)}, bf16[768,768]{1,0:T(8,128)(2,1)}, u32[]{:S(2)}, u32[]{:S(2)}) collective-permute-start(bf16[768,768]{1,0:T(8,128)(2,1)S(1)} %get-tuple-element.152), channel_id=1, source_target_pairs={{0,1},{1,0},{2,3},{3,2},{4,5},{5,4},{6,7},{7,6},{8,9},{9,8},{10,11... | collective-permute-start | bytes 3538952 | tf_op jit(solution)/shard_map/ppermute | solution.py:798
  9.7 21.2 %collective-permute-start.1 = (bf16[400,768]{1,0:T(8,128)(2,1)S(1)}, bf16[400,768]{1,0:T(8,128)(2,1)}, u32[]{:S(2)}, u32[]{:S(2)}) collective-permute-start(bf16[400,768]{1,0:T(8,128)(2,1)S(1)} %get-tuple-element.150), channel_id=1, source_target_pairs={{0,2},{1,3},{2,0},{3,1},{4,6},{5,7},{6,4},{7,5},{8,10},{9,11},{10,... | collective-permute-start | bytes 1843208 | tf_op jit(solution)/shard_map/ppermute | solution.py:798
  30.9 12.5 %collective-permute-start.3 = (bf16[400,768]{1,0:T(8,128)(2,1)}, bf16[400,768]{1,0:T(8,128)(2,1)S(1)}, u32[]{:S(2)}, u32[]{:S(2)}) collective-permute-start(bf16[400,768]{1,0:T(8,128)(2,1)} %collective-permute-done.1.near_ref.refs_3_.refs_5_.refs_11_), channel_id=1, source_target_pairs={{0,1},{1,0},{2,3},{3,2},{4,5},{5,4},{6,7},{7,6},{8,9},{9,8},{10,11... | collective-permute-start | bytes 1843208 | tf_op jit(solution)/shard_map/ppermute | solution.py:798
  31.3 17.7 %collective-permute-start.4 = (bf16[400,768]{1,0:T(8,128)(2,1)}, bf16[400,768]{1,0:T(8,128)(2,1)S(1)}, u32[]{:S(2)}, u32[]{:S(2)}) collective-permute-start(bf16[400,768]{1,0:T(8,128)(2,1)} %collective-permute-done.1.near_ref.refs_3_.refs_5_.refs_11_), channel_id=1, source_target_pairs={{0,4},{4,0},{8,12},{12,8},{16,20},{20,16},{24,28},{28,24},{1,5},{5... | collective-permute-start | bytes 1843208 | tf_op jit(solution)/shard_map/ppermute | solution.py:798
  32.8 16.2 %collective-permute-start.5 = (bf16[768,384]{1,0:T(8,128)(2,1)S(1)}, bf16[768,384]{1,0:T(8,128)(2,1)S(1)}, u32[]{:S(2)}, u32[]{:S(2)}) collective-permute-start(bf16[768,384]{1,0:T(8,128)(2,1)S(1)} %get-tuple-element.157), channel_id=1, source_target_pairs={{0,2},{1,3},{2,0},{3,1},{4,6},{5,7},{6,4},{7,5},{8,10},{9,11},{10,... | collective-permute-start | bytes 1769480 | tf_op jit(solution)/shard_map/ppermute | solution.py:798
  33.3 39.9 %collective-permute-start.7 = (bf16[768,768]{1,0:T(8,128)(2,1)S(1)}, bf16[768,768]{1,0:T(8,128)(2,1)S(1)}, u32[]{:S(2)}, u32[]{:S(2)}) collective-permute-start(bf16[768,768]{1,0:T(8,128)(2,1)S(1)} %copy-done.12), channel_id=1, source_target_pairs={{0,2},{1,3},{2,0},{3,1},{4,6},{5,7},{6,4},{7,5},{8,10},{9,11},{10,... | collective-permute-start | bytes 3538952 | tf_op jit(solution)/shard_map/ppermute | solution.py:798
  49.0 10.0 %collective-permute-start.6 = (bf16[400,768]{1,0:T(8,128)(2,1)S(1)}, bf16[400,768]{1,0:T(8,128)(2,1)S(1)}, u32[]{:S(2)}, u32[]{:S(2)}) collective-permute-start(bf16[400,768]{1,0:T(8,128)(2,1)S(1)} %collective-permute-done.4.refs_4_), channel_id=1, source_target_pairs={{0,1},{1,0},{2,3},{3,2},{4,5},{5,4},{6,7},{7,6},{8,9},{9,8},{10,11... | collective-permute-start | bytes 1843208 | tf_op jit(solution)/shard_map/ppermute | solution.py:798
  49.1 24.1 %collective-permute-start.8 = (bf16[768,384]{1,0:T(8,128)(2,1)S(1)}, bf16[768,384]{1,0:T(8,128)(2,1)S(1)}, u32[]{:S(2)}, u32[]{:S(2)}) collective-permute-start(bf16[768,384]{1,0:T(8,128)(2,1)S(1)} %collective-permute-done.5.refs_9_), channel_id=1, source_target_pairs={{0,4},{4,0},{8,12},{12,8},{16,20},{20,16},{24,28},{28,24},{1,5},{5... | collective-permute-start | bytes 1769480 | tf_op jit(solution)/shard_map/ppermute | solution.py:798
  108.8 53.4 %collective-permute-start.17 = (bf16[1536,768]{1,0:T(8,128)(2,1)S(1)}, bf16[1536,768]{1,0:T(8,128)(2,1)S(1)}, u32[]{:S(2)}, u32[]{:S(2)}) collective-permute-start(bf16[1536,768]{1,0:T(8,128)(2,1)S(1)} %add_convert_fusion), channel_id=1, source_target_pairs={{0,2},{1,3},{2,0},{3,1},{4,6},{5,7},{6,4},{7,5},{8,10},{9,11},{10,... | collective-permute-start | bytes 7077896 | tf_op jit(solution)/shard_map/ppermute | solution.py:798
  159.3 18.8 %collective-permute-start.18 = (bf16[768,768]{1,0:T(8,128)(2,1)}, bf16[768,768]{1,0:T(8,128)(2,1)S(1)}, u32[]{:S(2)}, u32[]{:S(2)}) collective-permute-start(bf16[768,768]{1,0:T(8,128)(2,1)} %get-tuple-element.201), channel_id=1, source_target_pairs={{0,1},{1,0},{2,3},{3,2},{4,5},{5,4},{6,7},{7,6},{8,9},{9,8},{10,11... | collective-permute-start | bytes 3538952 | tf_op jit(solution)/shard_map/ppermute | solution.py:798
  179.7 24.4 %collective-permute-start.19 = (bf16[768,768]{1,0:T(8,128)(2,1)}, bf16[768,768]{1,0:T(8,128)(2,1)S(1)}, u32[]{:S(2)}, u32[]{:S(2)}) collective-permute-start(bf16[768,768]{1,0:T(8,128)(2,1)} %get-tuple-element.212), channel_id=1, source_target_pairs={{0,1},{1,0},{2,3},{3,2},{4,5},{5,4},{6,7},{7,6},{8,9},{9,8},{10,11... | collective-permute-start | bytes 3538952 | tf_op jit(solution)/shard_map/ppermute | solution.py:798
  179.8 28.5 %collective-permute-start.20 = (bf16[768,768]{1,0:T(8,128)(2,1)S(1)}, bf16[768,768]{1,0:T(8,128)(2,1)}, u32[]{:S(2)}, u32[]{:S(2)}) collective-permute-start(bf16[768,768]{1,0:T(8,128)(2,1)S(1)} %add_convert_fusion.1), channel_id=1, source_target_pairs={{0,2},{1,3},{2,0},{3,1},{4,6},{5,7},{6,4},{7,5},{8,10},{9,11},{10,... | collective-permute-start | bytes 3538952 | tf_op jit(solution)/shard_map/ppermute | solution.py:798
  211.6 10.3 %collective-permute-start.22 = (bf16[192,768]{1,0:T(8,128)(2,1)S(1)}, bf16[192,768]{1,0:T(8,128)(2,1)S(1)}, u32[]{:S(2)}, u32[]{:S(2)}) collective-permute-start(bf16[192,768]{1,0:T(8,128)(2,1)S(1)} %get-tuple-element.231), channel_id=1, source_target_pairs={{0,8},{4,12},{8,0},{12,4},{16,24},{20,28},{24,16},{28,20},{1,9},{5... | collective-permute-start | bytes 884744 | tf_op jit(solution)/shard_map/ppermute | solution.py:798
  222.7 15.6 %collective-permute-start.23 = (bf16[96,768]{1,0:T(8,128)(2,1)S(1)}, bf16[96,768]{1,0:T(8,128)(2,1)S(1)}, u32[]{:S(2)}, u32[]{:S(2)}) collective-permute-start(bf16[96,768]{1,0:T(8,128)(2,1)S(1)} %get-tuple-element.232), channel_id=1, source_target_pairs={{0,8},{4,12},{8,0},{12,4},{16,24},{20,28},{24,16},{28,20},{1,9},{5... | collective-permute-start | bytes 442376 | tf_op jit(solution)/shard_map/ppermute | solution.py:798
  223.8 14.9 %collective-permute-start.24 = (bf16[96,768]{1,0:T(8,128)(2,1)S(1)}, bf16[96,768]{1,0:T(8,128)(2,1)S(1)}, u32[]{:S(2)}, u32[]{:S(2)}) collective-permute-start(bf16[96,768]{1,0:T(8,128)(2,1)S(1)} %get-tuple-element.233), channel_id=1, source_target_pairs={{0,16},{4,20},{8,24},{12,28},{16,0},{20,4},{24,8},{28,12},{1,17},{... | collective-permute-start | bytes 442376 | tf_op jit(solution)/shard_map/ppermute | solution.py:798
  240.3 11.9 %collective-permute-start.26 = (bf16[96,768]{1,0:T(8,128)(2,1)S(1)}, bf16[96,768]{1,0:T(8,128)(2,1)S(1)}, u32[]{:S(2)}, u32[]{:S(2)}) collective-permute-start(bf16[96,768]{1,0:T(8,128)(2,1)S(1)} %get-tuple-element.240.refs_0_), channel_id=1, source_target_pairs={{0,16},{4,20},{8,24},{12,28},{16,0},{20,4},{24,8},{28,12},{1,17},{... | collective-permute-start | bytes 442376 | tf_op jit(solution)/shard_map/ppermute | solution.py:798
  240.7 11.6 %collective-permute-start.27 = (bf16[96,768]{1,0:T(8,128)(2,1)S(1)}, bf16[96,768]{1,0:T(8,128)(2,1)S(1)}, u32[]{:S(2)}, u32[]{:S(2)}) collective-permute-start(bf16[96,768]{1,0:T(8,128)(2,1)S(1)} %get-tuple-element.241.refs_2_), channel_id=1, source_target_pairs={{0,4},{4,0},{8,12},{12,8},{16,20},{20,16},{24,28},{28,24},{1,5},{5... | collective-permute-start | bytes 442376 | tf_op jit(solution)/shard_map/ppermute | solution.py:798
  252.9 15.6 %collective-permute-start.29 = (bf16[96,768]{1,0:T(8,128)(2,1)S(1)}, bf16[96,768]{1,0:T(8,128)(2,1)S(1)}, u32[]{:S(2)}, u32[]{:S(2)}) collective-permute-start(bf16[96,768]{1,0:T(8,128)(2,1)S(1)} %get-tuple-element.245.refs_0_), channel_id=1, source_target_pairs={{0,8},{4,12},{8,0},{12,4},{16,24},{20,28},{24,16},{28,20},{1,9},{5... | collective-permute-start | bytes 442376 | tf_op jit(solution)/shard_map/ppermute | solution.py:798
  252.9 29.4 %collective-permute-start.30 = (bf16[96,768]{1,0:T(8,128)(2,1)S(1)}, bf16[96,768]{1,0:T(8,128)(2,1)S(1)}, u32[]{:S(2)}, u32[]{:S(2)}) collective-permute-start(bf16[96,768]{1,0:T(8,128)(2,1)S(1)} %get-tuple-element.249.refs_2_), channel_id=1, source_target_pairs={{0,16},{4,20},{8,24},{12,28},{16,0},{20,4},{24,8},{28,12},{1,17},{... | collective-permute-start | bytes 442376 | tf_op jit(solution)/shard_map/ppermute | solution.py:798
  257.1 25.2 %collective-permute-start.31 = (f32[24,768]{1,0:T(8,128)S(1)}, f32[24,768]{1,0:T(8,128)S(1)}, u32[]{:S(2)}, u32[]{:S(2)}) collective-permute-start(f32[24,768]{1,0:T(8,128)S(1)} %slice_add_fusion), channel_id=1, source_target_pairs={{0,4},{4,0},{8,12},{12,8},{16,20},{20,16},{24,28},{28,24},{1,5},{5... | collective-permute-start | bytes 221192 | tf_op jit(solution)/shard_map/ppermute | solution.py:798
  282.9 11.1 %collective-permute-start.32 = (bf16[192,768]{1,0:T(8,128)(2,1)S(1)}, bf16[192,768]{1,0:T(8,128)(2,1)S(1)}, u32[]{:S(2)}, u32[]{:S(2)}) collective-permute-start(bf16[192,768]{1,0:T(8,128)(2,1)S(1)} %get-tuple-element.253.refs_0_), channel_id=1, source_target_pairs={{0,4},{4,0},{8,12},{12,8},{16,20},{20,16},{24,28},{28,24},{1,5},{5... | collective-permute-start | bytes 884744 | tf_op jit(solution)/shard_map/ppermute | solution.py:798
  283.8 10.3 %collective-permute-start.33 = (bf16[192,768]{1,0:T(8,128)(2,1)S(1)}, bf16[192,768]{1,0:T(8,128)(2,1)S(1)}, u32[]{:S(2)}, u32[]{:S(2)}) collective-permute-start(bf16[192,768]{1,0:T(8,128)(2,1)S(1)} %get-tuple-element.254.refs_2_), channel_id=1, source_target_pairs={{0,8},{4,12},{8,0},{12,4},{16,24},{20,28},{24,16},{28,20},{1,9},{5... | collective-permute-start | bytes 884744 | tf_op jit(solution)/shard_map/ppermute | solution.py:798
  284.0 10.0 %collective-permute-start.34 = (f32[24,768]{1,0:T(8,128)S(1)}, f32[24,768]{1,0:T(8,128)S(1)}, u32[]{:S(2)}, u32[]{:S(2)}) collective-permute-start(f32[24,768]{1,0:T(8,128)S(1)} %add.47), channel_id=1, source_target_pairs={{0,8},{4,12},{8,0},{12,4},{16,24},{20,28},{24,16},{28,20},{1,9},{5... | collective-permute-start | bytes 221192 | tf_op jit(solution)/shard_map/ppermute | solution.py:798
  (44 other events, 432.9 us)
Sparse Core Ops, SparseCore 0:
  164.7 117.6 all-reduce.2

commit v2 on v1

--- a/solution.py
+++ b/solution.py
@@ -956,12 +956,12 @@
     return held, got
 
 
-def collect_kernel(ids_ref, sums2_ref, sums1_ref, tokens_ref, table0_ref, table1_ref, *refs):
+def collect_kernel(ids_ref, sums2_ref, sums1_ref, tokens_ref, table_ref, *refs):
     upb_refs, joint_refs, (out_ref, sent_ref) = refs[:2], refs[2:6], refs[6:]
     upb_lines = [upb_refs[1][8:16, :], upb_refs[1][0:8, :], upb_refs[0][8:16, :], upb_refs[0][0:8, :]]
     out_ref[...] = jnp.zeros_like(out_ref)
     sent_ref[...] = jnp.zeros_like(sent_ref)
-    table = table0_ref[...] + table1_ref[...]
+    table = table_ref[...]
 
     def total(values):
         return jnp.sum(values, axis=0, keepdims=True)
@@ -998,7 +998,7 @@
     return pl.pallas_call(
         collect_kernel,
         out_shape=(shaped((32, width), F32), shaped((32, width), F32)),
-        in_specs=[pl.BlockSpec(memory_space=pltpu.SMEM)] + [vmem] * 11,
+        in_specs=[pl.BlockSpec(memory_space=pltpu.SMEM)] + [vmem] * 10,
         out_specs=(vmem, vmem),
         cost_estimate=cost(1),
         name="collect",
@@ -1142,20 +1142,18 @@
     )
     totals = [(total0, 0), (total13, 0), (total2, 0), (total13, 1)]
     blocks = SEQ // TABLE_ROWS
-    table0 = table_sums(totals, index, chunks, 0, blocks // 2)
-    g0, r1, r2, table0 = lax.optimization_barrier((g0, r1, r2, table0))
+    table = table_sums(totals, index, chunks, 0, blocks)
+    held, sent = collect(
+        ids, sums2, sums1, token_images, [table], [upb32, upb10], [js0, js1, js2, js3]
+    )
+    g0, r1, r2, sent = lax.optimization_barrier((g0, r1, r2, sent))
     tail = Chain(dp_chain([g0, r1, r2], [3 * own, own]))
-    table1 = table_sums(totals, index, chunks, blocks // 2, blocks - blocks // 2)
-    held, sent = collect(
-        ids, sums2, sums1, token_images, [table0, table1], [upb32, upb10], [js0, js1, js2, js3]
-    )
-    tail.go_on()
     small = Chain(small_chain(held, sent, 16, 8))
     joint = 0
     while tail.done is None or small.done is None:
         going = [chain for chain in (tail, small) if chain.done is None]
         joint += 1
-        if joint == 3:
+        if joint == 4:
             going[0].got[0], up_sum, down_sum = lax.optimization_barrier(
                 (going[0].got[0], up_sum, down_sum)
             )

time: 313 us -> 308 us (0.984)
  waiting for transfers between devices: 73.4 us -> 67.4 us
    psum x1, waiting for transfers between devices: 13.9 us -> 9.76 us  [local(): up_sum, down_sum = lax.psum(tuple(mlp_sum), 'dp')]
    pallas_call x2 -> x1, Pallas kernels: 15.6 us -> 15.2 us  [table_sums(): pl.pallas_call(table_kernel, out_shape=shaped((chunks * heads, LANES), F3...]
    unnamed x63 -> x67, local copies, waits for them, and re-layouts: 8.37 us -> 8.14 us
  transfers between devices with their start and end apart: 37 -> 37, of which waited for: 16 -> 17; matrix products, arithmetic and copies ran while one was open for 6% -> 5% of each run, Pallas kernels for 47% -> 47%
where the time goes in v2:
time: 308 us; the launch traced here: 306 us
  Pallas kernels  169 us (55%)
  waiting for transfers between devices  67.4 us (22%)
  starting transfers between devices  30.8 us (10%)
  between operations  14.6 us (5%)
  local copies, waits for them, and re-layouts  12.2 us (4%)
  other arithmetic  11.6 us (4%)
    ppermute x36, waiting for transfers between devices, swap(): return lax.ppermute(values, axis, [(i, i ^ mask) for i in range(count)])  57.6 us
    pallas_call x3, Pallas kernels, attend_back(): pl.pallas_call(functools.partial(attend_back_kernel, first, last, count),...  48.2 us
    pallas_call x2, Pallas kernels, mlp(): pl.pallas_call(functools.partial(mlp_kernel, first, [len(shard) for shard...  40 us
    pallas_call x4, Pallas kernels, attend(): pl.pallas_call(functools.partial(attend_kernel, first, last, parted), out...  39.6 us
    ppermute x36, starting transfers between devices, swap(): return lax.ppermute(values, axis, [(i, i ^ mask) for i in range(count)])  30.8 us
    pallas_call x1, Pallas kernels, table_sums(): pl.pallas_call(table_kernel, out_shape=shaped((chunks * heads, LANES), F3...  15.2 us
    psum x1, waiting for transfers between devices, local(): up_sum, down_sum = lax.psum(tuple(mlp_sum), 'dp')  9.76 us
    unnamed x67, local copies, waits for them, and re-layouts  8.14 us
  transfers between devices with their start and end apart: 37, of which 17 were waited for; matrix products, arithmetic and copies ran while one was open for 5% of the time, Pallas kernels for 47%

profile of v2, /device:TPU:0, one launch (start us, length us, event | category | flops | bytes accessed | tf_op | source)
XLA Modules:
  0.0 306.1 jit_solution(3909181250455111481)
XLA Ops:
  16.9 3.4 %position_bias.2.refs_9_.refs_5_ = f32[6,200,256]{2,1,0:T(8,128)S(1)} custom-call(bf16[16,768]{1,0:T(8,128)(2,1)} %copy-done, bf16[16,768]{1,0:T(8,128)(2,1)} %copy-done.25, s32[200,200]{1,0:T(8,128)} %bitcast.35), custom_call_target="tpu_custom_call" | custom-call | flops 220000000 | tf_op jit(solution)/shard_map/position_bias/pallas_call | solution.py:194
  20.3 10.5 %attend.4 = (bf16[5,200,768]{2,1,0:T(8,128)(2,1)}, bf16[5,200,576]{2,1,0:T(8,128)(2,1)}, bf16[5,3,200,200]{3,2,1,0:T(8,128)(2,1)}, bf16[5,200,192]{2,1,0:T(8,128)(2,1)}, f32[5,200,768]{2,1,0:T(8,128)S(1)}) custom-call(s32[5]{0:T(128)S(1)} %dynamic_slice.6.refs_0_.ids_ref, bf16[5,200,768]{2,1,0:T(8,128)(2,1)} %bitcast.29, f32[8,200,1]{2,1,0:T(8,128)} %copy.50.refs_2_.refs_3_, ...), custom_call_target="tpu_custom_call" | custom-call | flops 990000000 | tf_op jit(solution)/shard_map/attend/pallas_call | solution.py:408
  34.8 8.5 %attend.5 = (bf16[5,200,576]{2,1,0:T(8,128)(2,1)}, bf16[5,3,200,200]{3,2,1,0:T(8,128)(2,1)}, bf16[5,200,192]{2,1,0:T(8,128)(2,1)}, f32[5,200,768]{2,1,0:T(8,128)S(1)}) custom-call(bf16[5,200,768]{2,1,0:T(8,128)(2,1)} %get-tuple-element.151.refs_0_.refs_1_.refs_9_.refs_2_.refs_7_, f32[5,200,768]{2,1,0:T(8,128)S(1)} %get-tuple-element.154.refs_1_, ...), custom_call_target="tpu_custom_call" | custom-call | flops 990000000 | tf_op jit(solution)/shard_map/attend/pallas_call | solution.py:408
  44.2 3.4 %position_bias.3.refs_6_.refs_14_ = f32[6,200,256]{2,1,0:T(8,128)S(1)} custom-call(bf16[400,768]{1,0:T(8,128)(2,1)} %copy-done.8, bf16[400,768]{1,0:T(8,128)(2,1)} %copy-done.9, s32[200,200]{1,0:T(8,128)} %bitcast.36), custom_call_target="tpu_custom_call" | custom-call | flops 220000000 | tf_op jit(solution)/shard_map/position_bias/pallas_call | solution.py:194
  49.8 9.1 %attend.6 = (bf16[5,200,576]{2,1,0:T(8,128)(2,1)}, bf16[5,3,200,200]{3,2,1,0:T(8,128)(2,1)}, bf16[5,200,192]{2,1,0:T(8,128)(2,1)}, f32[5,200,768]{2,1,0:T(8,128)S(1)}, bf16[768,768]{1,0:T(8,128)(2,1)}) custom-call(s32[1]{0:T(128)} %bitcast.side_ref.refs_0_.refs_1_, bf16[5,200,768]{2,1,0:T(8,128)(2,1)} %get-tuple-element.151.refs_0_.refs_1_.refs_9_.refs_2_.refs_7_, ...), custom_call_target="tpu_custom_call" | custom-call | flops 990000000 | tf_op jit(solution)/shard_map/attend/pallas_call | solution.py:408
  59.7 11.5 %attend.7 = (bf16[5,200,576]{2,1,0:T(8,128)(2,1)}, bf16[5,3,200,200]{3,2,1,0:T(8,128)(2,1)}, bf16[5,200,192]{2,1,0:T(8,128)(2,1)}, f32[5,200,768]{2,1,0:T(8,128)...) custom-call(s32[5]{0:T(128)S(1)} %dynamic_slice.6.refs_0_.ids_ref, ...), custom_call_target="tpu_custom_call" | custom-call | flops 990000000 | tf_op jit(solution)/shard_map/attend/pallas_call | solution.py:408
  73.8 3.1 %collective-permute-done.10.refs_5_ = bf16[768,384]{1,0:T(8,128)(2,1)S(1)} collective-permute-done((bf16[768,384]{1,0:T(8,128)(2,1)S(1)}, bf16[768,384]{1,0:T(8,128)(2,1)S(1)}, u32[]{:S(2)}, u32[]{:S(2)}) %collective-permute-start.10) | collective-permute-done | bytes 589856 | tf_op jit(solution)/shard_map/ppermute | solution.py:798
  79.6 20.0 %mlp.2 = (f32[1000,768]{1,0:T(8,128)S(1)}, f32[1000,768]{1,0:T(8,128)S(1)}, bf16[1536,768]{1,0:T(8,128)(2,1)}, bf16[1536,768]{1,0:T(8,128)(2,1)}, f32[16,768]{1,0:T(8,128)S(1)}) custom-call(s32[1]{0:T(128)} %bitcast.side_ref.refs_0_.refs_1_, bf16[1000,768]{1,0:T(8,128)(2,1)S(1)} %bitcast.26, bf16[1000,768]{1,0:T(8,128)(2,1)} %refs_2_.3, f32[768]{0:T(1024)} %gmlp_ref.1, ...), custom_call_target="tpu_custom_call" | custom-call | flops 1980000000 | tf_op jit(solution)/shard_map/mlp/pallas_call | solution.py:717
  100.3 6.1 %collective-permute-done.12 = bf16[1536,768]{1,0:T(8,128)(2,1)S(1)} collective-permute-done((bf16[1536,768]{1,0:T(8,128)(2,1)}, bf16[1536,768]{1,0:T(8,128)(2,1)S(1)}, u32[]{:S(2)}, u32[]{:S(2)}) %collective-permute-start.12) | collective-permute-done | bytes 2359328 | tf_op jit(solution)/shard_map/ppermute | solution.py:798
  110.7 20.1 %mlp.3 = (f32[1000,768]{1,0:T(8,128)S(1)}, f32[1000,768]{1,0:T(8,128)S(1)}, bf16[1536,768]{1,0:T(8,128)(2,1)}, bf16[1536,768]{1,0:T(8,128)(2,1)}, f32[16,768]{1,0:T(8,128)S(1)}) custom-call(s32[1]{0:T(128)} %bitcast.side_ref.refs_0_.refs_1_, bf16[1000,768]{1,0:T(8,128)(2,1)S(1)} %bitcast.27, ...), custom_call_target="tpu_custom_call", output_to_operand_aliasing={{0}: (10, {}), {1}: (11, {})} | custom-call | flops 1980000000 | tf_op jit(solution)/shard_map/mlp/pallas_call | solution.py:717
  133.2 6.7 %middle_back.1 = (bf16[5,200,768]{2,1,0:T(8,128)(2,1)}, f32[5,200,768]{2,1,0:T(8,128)}, bf16[5,200,768]{2,1,0:T(8,128)(2,1)}, f32[48,768]{1,0:T(8,128)S(1)}) custom-call(f32[5,200,768]{2,1,0:T(8,128)S(1)} %bitcast.24, f32[5,200,768]{2,1,0:T(8,128)S(1)} %bitcast.25, f32[5,200,768]{2,1,0:T(8,128)S(1)} %get-tuple-element.178.middle_ref, ...), custom_call_target="tpu_custom_call" | custom-call | flops 550000000 | tf_op jit(solution)/shard_map/middle_back/pallas_call | solution.py:779
  140.0 19.3 %attend_back.3 = (bf16[768,768]{1,0:T(8,128)(2,1)}, f32[8,576]{1,0:T(8,128)}, bf16[768,768]{1,0:T(8,128)(2,1)}, f32[8,576]{1,0:T(8,128)}, f32[6,200,200]{2,1,0:T(8,128)}, /*index=5*/f32[5,200,768]{2,1,0:T(8,128)}) custom-call(s32[5]{0:T(128)S(1)} %dynamic_slice.6.refs_0_.ids_ref, ...), custom_call_target="tpu_custom_call" | custom-call | flops 2860000000 | tf_op jit(solution)/shard_map/attend_back/pallas_call | solution.py:580
  164.5 13.5 %attend_back.4 = (bf16[768,768]{1,0:T(8,128)(2,1)}, f32[8,576]{1,0:T(8,128)}, f32[3,200,200]{2,1,0:T(8,128)}, f32[5,200,768]{2,1,0:T(8,128)}) custom-call(s32[5]{0:T(128)S(1)} %dynamic_slice.6.refs_0_.ids_ref, f32[5,200,768]{2,1,0:T(8,128)} %get-tuple-element.197.refs_1_, bf16[5,200,768]{2,1,0:T(8,128)(2,1)} %get-tuple-element.151.refs_0_.refs_1_.refs_9_.refs_2_.refs_7_, ...), custom_call_target="tpu_custom_call" | custom-call | flops 1430000000 | tf_op jit(solution)/shard_map/attend_back/pallas_call | solution.py:580
  180.6 15.4 %attend_back.5 = (bf16[768,768]{1,0:T(8,128)(2,1)}, f32[8,576]{1,0:T(8,128)}, f32[3,200,200]{2,1,0:T(8,128)}, f32[5,200,768]{2,1,0:T(8,128)}, f32[16,768]{1,0:T(8,128)S(1)}, /*index=5*/f32[5,8,768]{2,1,0:T(8,128)S(1)}) custom-call(s32[5]{0:T(128)S(1)} %dynamic_slice.6.refs_0_.ids_ref, bf16[5,200,768]{2,1,0:T(8,128)(2,1)} %bitcast.31, ...), custom_call_target="tpu_custom_call" | custom-call | flops 1430000000 | tf_op jit(solution)/shard_map/attend_back/pallas_call | solution.py:580
  196.0 15.2 %table_sums.1.table_ref = f32[72,128]{1,0:T(8,128)S(1)} custom-call(f32[3,200,200]{2,1,0:T(8,128)} %get-tuple-element.214.refs_0_, f32[6,200,200]{2,1,0:T(8,128)} %get-tuple-element.215.refs_1_.refs_3_, f32[3,200,200]{2,1,0:T(8,128)} %get-tuple-element.216.refs_2_, f32[6,200,200]{2,1,0:T(8,128)} %get-tuple-element.215.refs_1_.refs_3_, s32[200,200]{1,0:T(8,128)} %bitcast.37), custom_call_target="tpu_custom_call" | custom-call | flops 550000000 | tf_op jit(solution)/shard_map/table_sums/pallas_call | solution.py:233
  220.8 6.5 %collective-permute-done.21.refs_1_ = bf16[192,768]{1,0:T(8,128)(2,1)S(1)} collective-permute-done((bf16[192,768]{1,0:T(8,128)(2,1)S(1)}, bf16[192,768]{1,0:T(8,128)(2,1)S(1)}, u32[]{:S(2)}, u32[]{:S(2)}) %collective-permute-start.21) | collective-permute-done | bytes 294944 | tf_op jit(solution)/shard_map/ppermute | solution.py:798
  231.7 2.8 collective-permute-start.25
  245.7 6.3 %collective-permute-done.29 = f32[24,768]{1,0:T(8,128)S(1)} collective-permute-done((f32[24,768]{1,0:T(8,128)S(1)}, f32[24,768]{1,0:T(8,128)S(1)}, u32[]{:S(2)}, u32[]{:S(2)}) %collective-permute-start.29) | collective-permute-done | bytes 73760 | tf_op jit(solution)/shard_map/ppermute | solution.py:798
  252.0 6.5 %collective-permute-done.27.refs_1_ = bf16[96,768]{1,0:T(8,128)(2,1)S(1)} collective-permute-done((bf16[96,768]{1,0:T(8,128)(2,1)S(1)}, bf16[96,768]{1,0:T(8,128)(2,1)S(1)}, u32[]{:S(2)}, u32[]{:S(2)}) %collective-permute-start.27) | collective-permute-done | bytes 147488 | tf_op jit(solution)/shard_map/ppermute | solution.py:798
  259.2 2.9 collective-permute-start.31
  262.3 11.9 %collective-permute-done.30.refs_1_ = bf16[96,768]{1,0:T(8,128)(2,1)S(1)} collective-permute-done((bf16[96,768]{1,0:T(8,128)(2,1)S(1)}, bf16[96,768]{1,0:T(8,128)(2,1)S(1)}, u32[]{:S(2)}, u32[]{:S(2)}) %collective-permute-start.30) | collective-permute-done | bytes 147488 | tf_op jit(solution)/shard_map/ppermute | solution.py:798
  274.1 9.8 %all-reduce.3.cloned.1.call-done = (bf16[768,768]{1,0:T(8,128)(2,1)}, bf16[768,768]{1,0:T(8,128)(2,1)}) async-done(((bf16[768,768]{1,0:T(8,128)(2,1)}, bf16[768,768]{1,0:T(8,128)(2,1)}), (bf16[768,768]{1,0:T(8,128)(2,1)}, bf16[768,768]{1,0:T(8,128)(2,1)})) %all-reduce.3.cloned.1.call-update) | async-done | bytes 2359312 | tf_op jit(solution)/shard_map/psum | solution.py:1130
  286.1 3.0 collective-permute-start.35
  289.0 2.8 convert_element_type.66
  (159 shorter events, 73.4 us)
Async XLA Ops:
  7.2 276.7 %all-reduce.3.cloned.1.call-start = ((), (), s32[]{:S(2)}) async-start(), calls=%async_computation | async-start | bytes 4718592 | tf_op jit(solution)/shard_map/psum | solution.py:1130
  9.2 25.6 %collective-permute-start.2 = (bf16[768,768]{1,0:T(8,128)(2,1)S(1)}, bf16[768,768]{1,0:T(8,128)(2,1)}, u32[]{:S(2)}, u32[]{:S(2)}) collective-permute-start(bf16[768,768]{1,0:T(8,128)(2,1)S(1)} %get-tuple-element.155), channel_id=1, source_target_pairs={{0,1},{1,0},{2,3},{3,2},{4,5},{5,4},{6,7},{7,6},{8,9},{9,8},{10,11... | collective-permute-start | bytes 3538952 | tf_op jit(solution)/shard_map/ppermute | solution.py:798
  9.7 21.1 %collective-permute-start.1 = (bf16[400,768]{1,0:T(8,128)(2,1)S(1)}, bf16[400,768]{1,0:T(8,128)(2,1)S(1)}, u32[]{:S(2)}, u32[]{:S(2)}) collective-permute-start(bf16[400,768]{1,0:T(8,128)(2,1)S(1)} %get-tuple-element.153), channel_id=1, source_target_pairs={{0,2},{1,3},{2,0},{3,1},{4,6},{5,7},{6,4},{7,5},{8,10},{9,11},{10,... | collective-permute-start | bytes 1843208 | tf_op jit(solution)/shard_map/ppermute | solution.py:798
  30.9 12.4 %collective-permute-start.3 = (bf16[400,768]{1,0:T(8,128)(2,1)S(1)}, bf16[400,768]{1,0:T(8,128)(2,1)S(1)}, u32[]{:S(2)}, u32[]{:S(2)}) collective-permute-start(bf16[400,768]{1,0:T(8,128)(2,1)S(1)} %collective-permute-done.1.near_ref.refs_3_.refs_5_.refs_11_), channel_id=1, source_target_pairs={{0,1},{1,0},{2,3},{3,2},{4,5},{5,4},{6,7},{7,6},{8,9},{9,8},{10,11... | collective-permute-start | bytes 1843208 | tf_op jit(solution)/shard_map/ppermute | solution.py:798
  31.3 17.7 %collective-permute-start.4 = (bf16[400,768]{1,0:T(8,128)(2,1)S(1)}, bf16[400,768]{1,0:T(8,128)(2,1)S(1)}, u32[]{:S(2)}, u32[]{:S(2)}) collective-permute-start(bf16[400,768]{1,0:T(8,128)(2,1)S(1)} %collective-permute-done.1.near_ref.refs_3_.refs_5_.refs_11_), channel_id=1, source_target_pairs={{0,4},{4,0},{8,12},{12,8},{16,20},{20,16},{24,28},{28,24},{1,5},{5... | collective-permute-start | bytes 1843208 | tf_op jit(solution)/shard_map/ppermute | solution.py:798
  32.8 16.2 %collective-permute-start.5 = (bf16[768,384]{1,0:T(8,128)(2,1)S(1)}, bf16[768,384]{1,0:T(8,128)(2,1)S(1)}, u32[]{:S(2)}, u32[]{:S(2)}) collective-permute-start(bf16[768,384]{1,0:T(8,128)(2,1)S(1)} %get-tuple-element.160), channel_id=1, source_target_pairs={{0,2},{1,3},{2,0},{3,1},{4,6},{5,7},{6,4},{7,5},{8,10},{9,11},{10,... | collective-permute-start | bytes 1769480 | tf_op jit(solution)/shard_map/ppermute | solution.py:798
  33.3 39.9 %collective-permute-start.7 = (bf16[768,768]{1,0:T(8,128)(2,1)S(1)}, bf16[768,768]{1,0:T(8,128)(2,1)S(1)}, u32[]{:S(2)}, u32[]{:S(2)}) collective-permute-start(bf16[768,768]{1,0:T(8,128)(2,1)S(1)} %copy-done.12), channel_id=1, source_target_pairs={{0,2},{1,3},{2,0},{3,1},{4,6},{5,7},{6,4},{7,5},{8,10},{9,11},{10,... | collective-permute-start | bytes 3538952 | tf_op jit(solution)/shard_map/ppermute | solution.py:798
  49.0 9.9 %collective-permute-start.6 = (bf16[400,768]{1,0:T(8,128)(2,1)S(1)}, bf16[400,768]{1,0:T(8,128)(2,1)S(1)}, u32[]{:S(2)}, u32[]{:S(2)}) collective-permute-start(bf16[400,768]{1,0:T(8,128)(2,1)S(1)} %collective-permute-done.4.refs_4_), channel_id=1, source_target_pairs={{0,1},{1,0},{2,3},{3,2},{4,5},{5,4},{6,7},{7,6},{8,9},{9,8},{10,11... | collective-permute-start | bytes 1843208 | tf_op jit(solution)/shard_map/ppermute | solution.py:798
  49.1 24.1 %collective-permute-start.8 = (bf16[768,384]{1,0:T(8,128)(2,1)S(1)}, bf16[768,384]{1,0:T(8,128)(2,1)S(1)}, u32[]{:S(2)}, u32[]{:S(2)}) collective-permute-start(bf16[768,384]{1,0:T(8,128)(2,1)S(1)} %collective-permute-done.5.refs_9_), channel_id=1, source_target_pairs={{0,4},{4,0},{8,12},{12,8},{16,20},{20,16},{24,28},{28,24},{1,5},{5... | collective-permute-start | bytes 1769480 | tf_op jit(solution)/shard_map/ppermute | solution.py:798
  99.8 9.5 %collective-permute-start.13 = (bf16[768,768]{1,0:T(8,128)(2,1)S(1)}, bf16[768,768]{1,0:T(8,128)(2,1)S(1)}, u32[]{:S(2)}, u32[]{:S(2)}) collective-permute-start(bf16[768,768]{1,0:T(8,128)(2,1)S(1)} %copy-done.12), channel_id=1, source_target_pairs={{0,1},{1,0},{2,3},{3,2},{4,5},{5,4},{6,7},{7,6},{8,9},{9,8},{10,11... | collective-permute-start | bytes 3538952 | tf_op jit(solution)/shard_map/ppermute | solution.py:798
  108.8 53.4 %collective-permute-start.17 = (bf16[1536,768]{1,0:T(8,128)(2,1)S(1)}, bf16[1536,768]{1,0:T(8,128)(2,1)S(1)}, u32[]{:S(2)}, u32[]{:S(2)}) collective-permute-start(bf16[1536,768]{1,0:T(8,128)(2,1)S(1)} %add_convert_fusion), channel_id=1, source_target_pairs={{0,2},{1,3},{2,0},{3,1},{4,6},{5,7},{6,4},{7,5},{8,10},{9,11},{10,... | collective-permute-start | bytes 7077896 | tf_op jit(solution)/shard_map/ppermute | solution.py:798
  159.2 18.8 %collective-permute-start.18 = (bf16[768,768]{1,0:T(8,128)(2,1)}, bf16[768,768]{1,0:T(8,128)(2,1)S(1)}, u32[]{:S(2)}, u32[]{:S(2)}) collective-permute-start(bf16[768,768]{1,0:T(8,128)(2,1)} %get-tuple-element.204), channel_id=1, source_target_pairs={{0,1},{1,0},{2,3},{3,2},{4,5},{5,4},{6,7},{7,6},{8,9},{9,8},{10,11... | collective-permute-start | bytes 3538952 | tf_op jit(solution)/shard_map/ppermute | solution.py:798
  179.7 34.1 %collective-permute-start.19 = (bf16[768,768]{1,0:T(8,128)(2,1)}, bf16[768,768]{1,0:T(8,128)(2,1)S(1)}, u32[]{:S(2)}, u32[]{:S(2)}) collective-permute-start(bf16[768,768]{1,0:T(8,128)(2,1)} %get-tuple-element.225), channel_id=1, source_target_pairs={{0,1},{1,0},{2,3},{3,2},{4,5},{5,4},{6,7},{7,6},{8,9},{9,8},{10,11... | collective-permute-start | bytes 3538952 | tf_op jit(solution)/shard_map/ppermute | solution.py:798
  179.8 34.0 %collective-permute-start.20 = (bf16[768,768]{1,0:T(8,128)(2,1)S(1)}, bf16[768,768]{1,0:T(8,128)(2,1)}, u32[]{:S(2)}, u32[]{:S(2)}) collective-permute-start(bf16[768,768]{1,0:T(8,128)(2,1)S(1)} %add_convert_fusion.1), channel_id=1, source_target_pairs={{0,2},{1,3},{2,0},{3,1},{4,6},{5,7},{6,4},{7,5},{8,10},{9,11},{10,... | collective-permute-start | bytes 3538952 | tf_op jit(solution)/shard_map/ppermute | solution.py:798
  217.5 9.9 %collective-permute-start.21 = (bf16[192,768]{1,0:T(8,128)(2,1)S(1)}, bf16[192,768]{1,0:T(8,128)(2,1)S(1)}, u32[]{:S(2)}, u32[]{:S(2)}) collective-permute-start(bf16[192,768]{1,0:T(8,128)(2,1)S(1)} %get-tuple-element.231), channel_id=1, source_target_pairs={{0,4},{4,0},{8,12},{12,8},{16,20},{20,16},{24,28},{28,24},{1,5},{5... | collective-permute-start | bytes 884744 | tf_op jit(solution)/shard_map/ppermute | solution.py:798
  217.9 10.4 %collective-permute-start.22 = (bf16[192,768]{1,0:T(8,128)(2,1)S(1)}, bf16[192,768]{1,0:T(8,128)(2,1)S(1)}, u32[]{:S(2)}, u32[]{:S(2)}) collective-permute-start(bf16[192,768]{1,0:T(8,128)(2,1)S(1)} %get-tuple-element.232), channel_id=1, source_target_pairs={{0,8},{4,12},{8,0},{12,4},{16,24},{20,28},{24,16},{28,20},{1,9},{5... | collective-permute-start | bytes 884744 | tf_op jit(solution)/shard_map/ppermute | solution.py:798
  229.2 10.9 %collective-permute-start.24 = (bf16[96,768]{1,0:T(8,128)(2,1)S(1)}, bf16[96,768]{1,0:T(8,128)(2,1)S(1)}, u32[]{:S(2)}, u32[]{:S(2)}) collective-permute-start(bf16[96,768]{1,0:T(8,128)(2,1)S(1)} %get-tuple-element.239), channel_id=1, source_target_pairs={{0,8},{4,12},{8,0},{12,4},{16,24},{20,28},{24,16},{28,20},{1,9},{5... | collective-permute-start | bytes 442376 | tf_op jit(solution)/shard_map/ppermute | solution.py:798
  231.7 11.1 %collective-permute-start.25 = (bf16[96,768]{1,0:T(8,128)(2,1)S(1)}, bf16[96,768]{1,0:T(8,128)(2,1)S(1)}, u32[]{:S(2)}, u32[]{:S(2)}) collective-permute-start(bf16[96,768]{1,0:T(8,128)(2,1)S(1)} %get-tuple-element.240), channel_id=1, source_target_pairs={{0,16},{4,20},{8,24},{12,28},{16,0},{20,4},{24,8},{28,12},{1,17},{... | collective-permute-start | bytes 442376 | tf_op jit(solution)/shard_map/ppermute | solution.py:798
  243.5 15.0 %collective-permute-start.27 = (bf16[96,768]{1,0:T(8,128)(2,1)S(1)}, bf16[96,768]{1,0:T(8,128)(2,1)S(1)}, u32[]{:S(2)}, u32[]{:S(2)}) collective-permute-start(bf16[96,768]{1,0:T(8,128)(2,1)S(1)} %get-tuple-element.246.refs_0_), channel_id=1, source_target_pairs={{0,16},{4,20},{8,24},{12,28},{16,0},{20,4},{24,8},{28,12},{1,17},{... | collective-permute-start | bytes 442376 | tf_op jit(solution)/shard_map/ppermute | solution.py:798
  243.5 15.0 %collective-permute-start.28 = (bf16[96,768]{1,0:T(8,128)(2,1)S(1)}, bf16[96,768]{1,0:T(8,128)(2,1)S(1)}, u32[]{:S(2)}, u32[]{:S(2)}) collective-permute-start(bf16[96,768]{1,0:T(8,128)(2,1)S(1)} %get-tuple-element.247.refs_2_), channel_id=1, source_target_pairs={{0,4},{4,0},{8,12},{12,8},{16,20},{20,16},{24,28},{28,24},{1,5},{5... | collective-permute-start | bytes 442376 | tf_op jit(solution)/shard_map/ppermute | solution.py:798
  259.1 15.0 %collective-permute-start.30 = (bf16[96,768]{1,0:T(8,128)(2,1)S(1)}, bf16[96,768]{1,0:T(8,128)(2,1)S(1)}, u32[]{:S(2)}, u32[]{:S(2)}) collective-permute-start(bf16[96,768]{1,0:T(8,128)(2,1)S(1)} %get-tuple-element.251.refs_0_), channel_id=1, source_target_pairs={{0,8},{4,12},{8,0},{12,4},{16,24},{20,28},{24,16},{28,20},{1,9},{5... | collective-permute-start | bytes 442376 | tf_op jit(solution)/shard_map/ppermute | solution.py:798
  259.2 24.7 %collective-permute-start.31 = (bf16[96,768]{1,0:T(8,128)(2,1)S(1)}, bf16[96,768]{1,0:T(8,128)(2,1)S(1)}, u32[]{:S(2)}, u32[]{:S(2)}) collective-permute-start(bf16[96,768]{1,0:T(8,128)(2,1)S(1)} %get-tuple-element.255.refs_2_), channel_id=1, source_target_pairs={{0,16},{4,20},{8,24},{12,28},{16,0},{20,4},{24,8},{28,12},{1,17},{... | collective-permute-start | bytes 442376 | tf_op jit(solution)/shard_map/ppermute | solution.py:798
  262.1 21.8 %collective-permute-start.32 = (f32[24,768]{1,0:T(8,128)S(1)}, f32[24,768]{1,0:T(8,128)S(1)}, u32[]{:S(2)}, u32[]{:S(2)}) collective-permute-start(f32[24,768]{1,0:T(8,128)S(1)} %add.47), channel_id=1, source_target_pairs={{0,8},{4,12},{8,0},{12,4},{16,24},{20,28},{24,16},{28,20},{1,9},{5... | collective-permute-start | bytes 221192 | tf_op jit(solution)/shard_map/ppermute | solution.py:798
  285.6 9.8 %collective-permute-start.34 = (bf16[192,768]{1,0:T(8,128)(2,1)S(1)}, bf16[192,768]{1,0:T(8,128)(2,1)S(1)}, u32[]{:S(2)}, u32[]{:S(2)}) collective-permute-start(bf16[192,768]{1,0:T(8,128)(2,1)S(1)} %get-tuple-element.260.refs_2_), channel_id=1, source_target_pairs={{0,8},{4,12},{8,0},{12,4},{16,24},{20,28},{24,16},{28,20},{1,9},{5... | collective-permute-start | bytes 884744 | tf_op jit(solution)/shard_map/ppermute | solution.py:798
  (46 other events, 478.7 us)
Sparse Core Ops, SparseCore 0:
  164.7 119.1 all-reduce.2
